TPU v7x, 512 devices: a whole 4x4x16 slice. The times are simulated.
512 devices in a mesh: row: 32 (over y_hi, z), col: 16 (over x, y_lo, core).
Axes of the slice: x: 4, y: 4 (y_hi: 2, y_lo: 2; y = y_hi * 2 + y_lo), z: 16, core: 2. Of those that a mesh axis runs over, the one named last changes fastest.
Arguments:
- left_blocks: float32 [32, 32, 4, 4096], P('row', 'col'), may hold values from -0.75 to 0.75
- right_blocks: float32 [32, 16, 20, 4096], P('row', 'col'), may hold values from -6 to 6
- left_slots: int32 [32, 16, 4, 2, 24], P('row', 'col'), may hold values from 0 to 3
- right_slots: int32 [32, 16, 4, 2, 24], P('row', 'col'), may hold values from 0 to 19
- sink_slots: int32 [32, 16, 4, 2, 24], P('row', 'col'), may hold values from 0 to 11
- live_counts: int32 [32, 16, 4, 2], P('row', 'col'), may hold values from 3 to 24, as said below
Outputs:
- product_blocks: float32 [32, 16, 12, 4096], P('row', 'col')
Inputs may be any that keep to these rules, and one draw needn't show every extreme that they name: `live_counts`: entries of a list at positions from its live count on are not read; at least one list in every draw is full.
All inputs are finite; a program needn't handle non-finite values.
Results may differ from a plain program's by a relative error of at most 0.0003.
Values sent between devices are 32-bit elements; how exact they have to be, the bound alone decides.
A program may use at most 64 MiB of HBM per device.

v0:
```python
import jax
import jax.numpy as jnp
from jax import lax
from jax.sharding import PartitionSpec as P

TILE_SIDE = 64
SINK_SLOTS = 12
PRODUCTS = 24
SECTIONS = 4


def shifted_2(shard, axis, by):
    devices = lax.axis_size(axis)
    return lax.ppermute(shard, axis, [(i, (i + by) % devices) for i in range(devices)])


def partner_2(value, axis, apart):
    mask = 2**apart
    pairs = [(source, source ^ mask) for source in range(lax.axis_size(axis))]
    return lax.ppermute(value, axis, pairs)


def block_terms(running, left_panel, right_panel, left_index, right_index, sink_index, live_count):
    is_live = (jnp.arange(PRODUCTS) < live_count).astype(jnp.float32)
    left_tiles = jnp.take(left_panel, left_index, axis=0).reshape(PRODUCTS, TILE_SIDE, TILE_SIDE)
    right_tiles = jnp.take(right_panel, right_index, axis=0).reshape(PRODUCTS, TILE_SIDE, TILE_SIDE)
    products = jnp.einsum("pik,pkj->pij", left_tiles, right_tiles, precision=lax.Precision.HIGHEST)
    products = products.reshape(PRODUCTS, TILE_SIDE * TILE_SIDE)
    sink_table = (jnp.arange(SINK_SLOTS)[:, None] == sink_index[None, :]).astype(
        jnp.float32
    ) * is_live[None, :]
    return running + jnp.dot(
        sink_table, products, precision=lax.Precision.HIGHEST, preferred_element_type=jnp.float32
    )


def order_pair(own_panel, partner, parity):
    first_half = jnp.where(parity == 0, own_panel, partner)
    second_half = jnp.where(parity == 0, partner, own_panel)
    return jnp.stack([first_half, second_half])


def per_device(left_blocks, right_blocks, left_slots, right_slots, sink_slots, live_counts):
    col_count = lax.axis_size("col")
    col_bits = col_count.bit_length() - 1
    half_row = lax.axis_index("row") // 2
    parity = lax.axis_index("row") % 2
    column = lax.axis_index("col")
    left_lists = left_slots[0, 0]
    right_lists = right_slots[0, 0]
    sink_lists = sink_slots[0, 0]
    count_lists = live_counts[0, 0]
    own_panel = right_blocks[0, 0]
    for bit_no in range(col_bits):
        shifted = shifted_2(own_panel, "row", -(2 << bit_no))
        own_panel = jnp.where(column // (1 << bit_no) % 2 == 1, shifted, own_panel)
    right_pairs = []
    for section_no in range(SECTIONS):
        partner = partner_2(own_panel, "row", 0)
        right_pairs.append(order_pair(own_panel, partner, parity))
        if section_no + 1 < SECTIONS:
            own_panel = shifted_2(own_panel, "row", -2)
    running = jnp.zeros((SINK_SLOTS, TILE_SIDE * TILE_SIDE), jnp.float32)
    left_pair = left_blocks[0]
    for bit_no in range(col_bits):
        shifted = shifted_2(left_pair, "col", -(1 << bit_no))
        left_pair = jnp.where(half_row // (1 << bit_no) % 2 == 1, shifted, left_pair)
    for section_no in range(SECTIONS):
        for half_no in range(2):
            running = block_terms(
                running,
                left_pair[half_no],
                right_pairs[section_no][half_no],
                left_lists[section_no, half_no],
                right_lists[section_no, half_no],
                sink_lists[section_no, half_no],
                count_lists[section_no, half_no],
            )
        if section_no + 1 < SECTIONS:
            left_pair = shifted_2(left_pair, "col", -1)
    return running[None, None]


def solution(mesh):
    return jax.shard_map(
        per_device,
        mesh=mesh,
        in_specs=(
            P("row", "col", None, None),
            P("row", "col", None, None),
            P("row", "col", None, None, None),
            P("row", "col", None, None, None),
            P("row", "col", None, None, None),
            P("row", "col", None, None),
        ),
        out_specs=P("row", "col", None, None),
        check_vma=False,
    )
```

profile of v0, /device:TPU:146, one launch (start us, length us, event | category | flops | bytes accessed | tf_op | source)
XLA Modules:
  0.0 274.4 jit_solution(12531519113850311531)
XLA Ops:
  0.0 2.6 collective-permute-start
  3.8 2.1 collective-permute-start.4
  16.8 2.7 collective-permute-start.1
  21.2 2.7 collective-permute-done.1
  23.9 4.4 %collective-permute-start.2 = (f32[2,4,4096]{2,1,0:T(4,128)S(1)}, f32[2,4,4096]{2,1,0:T(4,128)S(1)}, u32[]{:S(2)}, u32[]{:S(2)}) collective-permute-start(f32[2,4,4096]{2,1,0:T(4,128)S(1)} %bitcast.166), channel_id=1, source_target_pairs={{0,12},{1,13},{2,14},{3,15},{4,0},{5,1},{6,2},{7,3},{8,4},{9,5},{1... | collective-permute-start | bytes 393224 | tf_op jit(solution)/shard_map/ppermute | solution.py:14
  30.8 5.2 %collective-permute-start.3 = (f32[2,4,4096]{2,1,0:T(4,128)S(1)}, f32[2,4,4096]{2,1,0:T(4,128)S(1)}, u32[]{:S(2)}, u32[]{:S(2)}) collective-permute-start(f32[2,4,4096]{2,1,0:T(4,128)S(1)} %bitcast.170), channel_id=1, source_target_pairs={{0,8},{1,9},{2,10},{3,11},{4,12},{5,13},{6,14},{7,15},{8,0},{9,1},... | collective-permute-start | bytes 393224 | tf_op jit(solution)/shard_map/ppermute | solution.py:14
  36.3 10.6 %collective-permute-start.5 = (f32[20,4096]{1,0:T(8,128)S(1)}, f32[20,4096]{1,0:T(8,128)S(1)}, u32[]{:S(2)}, u32[]{:S(2)}) collective-permute-start(f32[20,4096]{1,0:T(8,128)S(1)} %broadcast_select_fusion.16), channel_id=1, source_target_pairs={{0,448},{16,464},{32,480},{48,496},{64,0},{80,16},{96,32},{112,48}... | collective-permute-start | bytes 983048 | tf_op jit(solution)/shard_map/ppermute | solution.py:14
  47.0 2.3 collective-permute-start.9
  53.2 19.1 %collective-permute-done.5 = f32[20,4096]{1,0:T(8,128)S(1)} collective-permute-done((f32[20,4096]{1,0:T(8,128)S(1)}, f32[20,4096]{1,0:T(8,128)S(1)}, u32[]{:S(2)}, u32[]{:S(2)}) %collective-permute-start.5) | collective-permute-done | bytes 327712 | tf_op jit(solution)/shard_map/ppermute | solution.py:14
  72.4 11.6 %collective-permute-start.6 = (f32[20,4096]{1,0:T(8,128)S(1)}, f32[20,4096]{1,0:T(8,128)S(1)}, u32[]{:S(2)}, u32[]{:S(2)}) collective-permute-start(f32[20,4096]{1,0:T(8,128)S(1)} %broadcast_select_fusion.17), channel_id=1, source_target_pairs={{0,384},{16,400},{32,416},{48,432},{64,448},{80,464},{96,480},{112... | collective-permute-start | bytes 983048 | tf_op jit(solution)/shard_map/ppermute | solution.py:14
  85.3 10.4 %collective-permute-start.12 = (f32[2,4,4096]{2,1,0:T(4,128)S(1)}, f32[2,4,4096]{2,1,0:T(4,128)S(1)}, u32[]{:S(2)}, u32[]{:S(2)}) collective-permute-start(f32[2,4,4096]{2,1,0:T(4,128)S(1)} %collective-permute-done.9), channel_id=1, source_target_pairs={{0,15},{1,0},{2,1},{3,2},{4,3},{5,4},{6,5},{7,6},{8,7},{9,8},{10,9... | collective-permute-start | bytes 393224 | tf_op jit(solution)/shard_map/ppermute | solution.py:14
  101.3 4.9 %collective-permute-start.15 = (f32[2,4,4096]{2,1,0:T(4,128)S(1)}, f32[2,4,4096]{2,1,0:T(4,128)S(1)}, u32[]{:S(2)}, u32[]{:S(2)}) collective-permute-start(f32[2,4,4096]{2,1,0:T(4,128)S(1)} %collective-permute-done.12), channel_id=1, source_target_pairs={{0,15},{1,0},{2,1},{3,2},{4,3},{5,4},{6,5},{7,6},{8,7},{9,8},{10,9... | collective-permute-start | bytes 393224 | tf_op jit(solution)/shard_map/ppermute | solution.py:14
  111.3 11.1 %collective-permute-done.7 = f32[20,4096]{1,0:T(8,128)S(1)} collective-permute-done((f32[20,4096]{1,0:T(8,128)S(1)}, f32[20,4096]{1,0:T(8,128)S(1)}, u32[]{:S(2)}, u32[]{:S(2)}) %collective-permute-start.7) | collective-permute-done | bytes 327712 | tf_op jit(solution)/shard_map/ppermute | solution.py:14
  126.5 14.0 %collective-permute-start.10 = (f32[20,4096]{1,0:T(8,128)}, f32[20,4096]{1,0:T(8,128)}, u32[]{:S(2)}, u32[]{:S(2)}) collective-permute-start(f32[20,4096]{1,0:T(8,128)} %broadcast_select_fusion.19), channel_id=1, source_target_pairs={{0,480},{16,496},{32,0},{48,16},{64,32},{80,48},{96,64},{112,80},{... | collective-permute-start | bytes 983048 | tf_op jit(solution)/shard_map/ppermute | solution.py:14
  148.6 2.9 %fusion.43 = f32[24,64,64]{2,1,0:T(8,128)} fusion(f32[24,64,64]{2,1,0:T(8,128)S(1)} %copy-done.4, f32[24,64,64]{2,1,0:T(8,128)} %reshape.131), kind=kOutput, calls=%fused_computation.195 | convolution fusion | flops 75497472 | bytes 1179648 | tf_op jit(solution)/shard_map/pik,pkj->pij/dot_general | solution.py:27
  153.0 2.3 reshape.134
  155.3 2.9 %fusion.44 = f32[24,64,64]{2,1,0:T(8,128)} fusion(f32[24,64,64]{2,1,0:T(8,128)S(1)} %copy-done.3, f32[24,64,64]{2,1,0:T(8,128)} %reshape.134), kind=kOutput, calls=%fused_computation.196 | convolution fusion | flops 75497472 | bytes 1179648 | tf_op jit(solution)/shard_map/pik,pkj->pij/dot_general | solution.py:27
  158.2 9.2 %collective-permute-done.10 = f32[20,4096]{1,0:T(8,128)} collective-permute-done((f32[20,4096]{1,0:T(8,128)}, f32[20,4096]{1,0:T(8,128)}, u32[]{:S(2)}, u32[]{:S(2)}) %collective-permute-start.10) | collective-permute-done | bytes 327712 | tf_op jit(solution)/shard_map/ppermute | solution.py:14
  167.4 11.7 %collective-permute-start.11 = (f32[20,4096]{1,0:T(8,128)}, f32[20,4096]{1,0:T(8,128)}, u32[]{:S(2)}, u32[]{:S(2)}) collective-permute-start(f32[20,4096]{1,0:T(8,128)} %collective-permute-done.10), channel_id=1, source_target_pairs={{0,16},{16,0},{32,48},{48,32},{64,80},{80,64},{96,112},{112,96},{1... | collective-permute-start | bytes 983048 | tf_op jit(solution)/shard_map/ppermute | solution.py:20
  180.9 2.1 collective-permute-start.13
  184.1 13.7 %collective-permute-done.11 = f32[20,4096]{1,0:T(8,128)} collective-permute-done((f32[20,4096]{1,0:T(8,128)}, f32[20,4096]{1,0:T(8,128)}, u32[]{:S(2)}, u32[]{:S(2)}) %collective-permute-start.11) | collective-permute-done | bytes 327712 | tf_op jit(solution)/shard_map/ppermute | solution.py:20
  205.5 2.9 %fusion.45 = f32[24,64,64]{2,1,0:T(8,128)} fusion(f32[24,64,64]{2,1,0:T(8,128)S(1)} %copy-done.2, f32[24,64,64]{2,1,0:T(8,128)} %reshape.137), kind=kOutput, calls=%fused_computation.197 | convolution fusion | flops 75497472 | bytes 1179648 | tf_op jit(solution)/shard_map/pik,pkj->pij/dot_general | solution.py:27
  209.9 2.3 reshape.140
  212.2 3.0 %fusion.46 = f32[24,64,64]{2,1,0:T(8,128)} fusion(f32[24,64,64]{2,1,0:T(8,128)S(1)} %copy-done.1, f32[24,64,64]{2,1,0:T(8,128)} %reshape.140), kind=kOutput, calls=%fused_computation.198 | convolution fusion | flops 75497472 | bytes 1179648 | tf_op jit(solution)/shard_map/pik,pkj->pij/dot_general | solution.py:27
  215.1 2.0 collective-permute-start.14
  218.6 1.9 collective-permute-start.16
  220.5 2.0 convolution_add_fusion.4
  222.5 15.4 %collective-permute-done.14 = f32[20,4096]{1,0:T(8,128)} collective-permute-done((f32[20,4096]{1,0:T(8,128)}, f32[20,4096]{1,0:T(8,128)}, u32[]{:S(2)}, u32[]{:S(2)}) %collective-permute-start.14) | collective-permute-done | bytes 327712 | tf_op jit(solution)/shard_map/ppermute | solution.py:20
  245.6 2.9 %fusion.47 = f32[24,64,64]{2,1,0:T(8,128)} fusion(f32[24,64,64]{2,1,0:T(8,128)S(1)} %copy-done, f32[24,64,64]{2,1,0:T(8,128)} %reshape.143), kind=kOutput, calls=%fused_computation.199 | convolution fusion | flops 75497472 | bytes 1179648 | tf_op jit(solution)/shard_map/pik,pkj->pij/dot_general | solution.py:27
  251.3 2.1 fusion.48
  253.4 2.1 collective-permute-start.17
  258.0 5.4 %collective-permute-done.17 = f32[20,4096]{1,0:T(8,128)} collective-permute-done((f32[20,4096]{1,0:T(8,128)}, f32[20,4096]{1,0:T(8,128)}, u32[]{:S(2)}, u32[]{:S(2)}) %collective-permute-start.17) | collective-permute-done | bytes 327712 | tf_op jit(solution)/shard_map/ppermute | solution.py:20
  (206 shorter events, 82.9 us)
Async XLA Ops:
  0.0 16.7 %collective-permute-start = (f32[2,4,4096]{2,1,0:T(4,128)}, f32[2,4,4096]{2,1,0:T(4,128)S(1)}, u32[]{:S(2)}, u32[]{:S(2)}) collective-permute-start(f32[2,4,4096]{2,1,0:T(4,128)} %bitcast.172), channel_id=1, source_target_pairs={{0,15},{1,0},{2,1},{3,2},{4,3},{5,4},{6,5},{7,6},{8,7},{9,8},{10,9... | collective-permute-start | bytes 393224 | tf_op jit(solution)/shard_map/ppermute | solution.py:14
  2.6 3.3 %copy-start.17 = (s32[1,1,4,2,24]{4,3,2,1,0:T(2,128)S(1)}, s32[1,1,4,2,24]{4,3,2,1,0:T(2,128)}, u32[]{:S(2)}) copy-start(s32[1,1,4,2,24]{4,3,2,1,0:T(2,128)} %param.12) | copy-start | bytes 2308
  2.6 3.9 %copy-start.18 = (s32[1,1,4,2,24]{4,3,2,1,0:T(2,128)S(1)}, s32[1,1,4,2,24]{4,3,2,1,0:T(2,128)}, u32[]{:S(2)}) copy-start(s32[1,1,4,2,24]{4,3,2,1,0:T(2,128)} %param.13) | copy-start | bytes 2308
  2.6 5.7 %copy-start.16 = (s32[1,1,4,2]{2,3,1,0:T(2,128)S(1)}, s32[1,1,4,2]{2,3,1,0:T(2,128)}, u32[]{:S(2)}) copy-start(s32[1,1,4,2]{2,3,1,0:T(2,128)} %param.15) | copy-start | bytes 100
  2.6 7.6 %copy-start.19 = (s32[1,1,4,2,24]{4,3,2,1,0:T(2,128)S(1)}, s32[1,1,4,2,24]{4,3,2,1,0:T(2,128)}, u32[]{:S(2)}) copy-start(s32[1,1,4,2,24]{4,3,2,1,0:T(2,128)} %param.14) | copy-start | bytes 2308
  3.8 12.9 %copy-start.15 = (f32[1,2,4,4096]{3,2,1,0:T(4,128)S(1)}, f32[1,2,4,4096]{3,2,1,0:T(4,128)}, u32[]{:S(2)}) copy-start(f32[1,2,4,4096]{3,2,1,0:T(4,128)} %param.10) | copy-start | bytes 393220
  3.8 32.2 %collective-permute-start.4 = (f32[20,4096]{1,0:T(8,128)S(1)}, f32[20,4096]{1,0:T(8,128)S(1)}, u32[]{:S(2)}, u32[]{:S(2)}) collective-permute-start(f32[20,4096]{1,0:T(8,128)S(1)} %bitcast.171), channel_id=1, source_target_pairs={{0,480},{16,496},{32,0},{48,16},{64,32},{80,48},{96,64},{112,80},{... | collective-permute-start | bytes 983048 | tf_op jit(solution)/shard_map/ppermute | solution.py:14
  16.8 7.1 %collective-permute-start.1 = (f32[2,4,4096]{2,1,0:T(4,128)S(1)}, f32[2,4,4096]{2,1,0:T(4,128)S(1)}, u32[]{:S(2)}, u32[]{:S(2)}) collective-permute-start(f32[2,4,4096]{2,1,0:T(4,128)S(1)} %broadcast_select_fusion.28), channel_id=1, source_target_pairs={{0,14},{1,15},{2,0},{3,1},{4,2},{5,3},{6,4},{7,5},{8,6},{9,7},{10,... | collective-permute-start | bytes 393224 | tf_op jit(solution)/shard_map/ppermute | solution.py:14
  23.9 6.9 %collective-permute-start.2 = (f32[2,4,4096]{2,1,0:T(4,128)S(1)}, f32[2,4,4096]{2,1,0:T(4,128)S(1)}, u32[]{:S(2)}, u32[]{:S(2)}) collective-permute-start(f32[2,4,4096]{2,1,0:T(4,128)S(1)} %bitcast.166), channel_id=1, source_target_pairs={{0,12},{1,13},{2,14},{3,15},{4,0},{5,1},{6,2},{7,3},{8,4},{9,5},{1... | collective-permute-start | bytes 393224 | tf_op jit(solution)/shard_map/ppermute | solution.py:14
  29.6 6.5 %copy-start.11 = (f32[1,1,20,4096]{3,1,2,0:T(1,128)S(1)}, f32[1,1,20,4096]{3,1,2,0:T(1,128)}, u32[]{:S(2)}) copy-start(f32[1,1,20,4096]{3,1,2,0:T(1,128)} %param.11) | copy-start | bytes 983044
  30.8 16.1 %collective-permute-start.3 = (f32[2,4,4096]{2,1,0:T(4,128)S(1)}, f32[2,4,4096]{2,1,0:T(4,128)S(1)}, u32[]{:S(2)}, u32[]{:S(2)}) collective-permute-start(f32[2,4,4096]{2,1,0:T(4,128)S(1)} %bitcast.170), channel_id=1, source_target_pairs={{0,8},{1,9},{2,10},{3,11},{4,12},{5,13},{6,14},{7,15},{8,0},{9,1},... | collective-permute-start | bytes 393224 | tf_op jit(solution)/shard_map/ppermute | solution.py:14
  36.3 36.0 %collective-permute-start.5 = (f32[20,4096]{1,0:T(8,128)S(1)}, f32[20,4096]{1,0:T(8,128)S(1)}, u32[]{:S(2)}, u32[]{:S(2)}) collective-permute-start(f32[20,4096]{1,0:T(8,128)S(1)} %broadcast_select_fusion.16), channel_id=1, source_target_pairs={{0,448},{16,464},{32,480},{48,496},{64,0},{80,16},{96,32},{112,48}... | collective-permute-start | bytes 983048 | tf_op jit(solution)/shard_map/ppermute | solution.py:14
  47.0 36.9 %collective-permute-start.9 = (f32[2,4,4096]{2,1,0:T(4,128)S(1)}, f32[2,4,4096]{2,1,0:T(4,128)S(1)}, u32[]{:S(2)}, u32[]{:S(2)}) collective-permute-start(f32[2,4,4096]{2,1,0:T(4,128)S(1)} %bitcast.169), channel_id=1, source_target_pairs={{0,15},{1,0},{2,1},{3,2},{4,3},{5,4},{6,5},{7,6},{8,7},{9,8},{10,9... | collective-permute-start | bytes 393224 | tf_op jit(solution)/shard_map/ppermute | solution.py:14
  72.4 35.6 %collective-permute-start.6 = (f32[20,4096]{1,0:T(8,128)S(1)}, f32[20,4096]{1,0:T(8,128)S(1)}, u32[]{:S(2)}, u32[]{:S(2)}) collective-permute-start(f32[20,4096]{1,0:T(8,128)S(1)} %broadcast_select_fusion.17), channel_id=1, source_target_pairs={{0,384},{16,400},{32,416},{48,432},{64,448},{80,464},{96,480},{112... | collective-permute-start | bytes 983048 | tf_op jit(solution)/shard_map/ppermute | solution.py:14
  85.3 13.0 %collective-permute-start.12 = (f32[2,4,4096]{2,1,0:T(4,128)S(1)}, f32[2,4,4096]{2,1,0:T(4,128)S(1)}, u32[]{:S(2)}, u32[]{:S(2)}) collective-permute-start(f32[2,4,4096]{2,1,0:T(4,128)S(1)} %collective-permute-done.9), channel_id=1, source_target_pairs={{0,15},{1,0},{2,1},{3,2},{4,3},{5,4},{6,5},{7,6},{8,7},{9,8},{10,9... | collective-permute-start | bytes 393224 | tf_op jit(solution)/shard_map/ppermute | solution.py:14
  101.3 8.6 %collective-permute-start.15 = (f32[2,4,4096]{2,1,0:T(4,128)S(1)}, f32[2,4,4096]{2,1,0:T(4,128)S(1)}, u32[]{:S(2)}, u32[]{:S(2)}) collective-permute-start(f32[2,4,4096]{2,1,0:T(4,128)S(1)} %collective-permute-done.12), channel_id=1, source_target_pairs={{0,15},{1,0},{2,1},{3,2},{4,3},{5,4},{6,5},{7,6},{8,7},{9,8},{10,9... | collective-permute-start | bytes 393224 | tf_op jit(solution)/shard_map/ppermute | solution.py:14
  108.0 14.4 %collective-permute-start.7 = (f32[20,4096]{1,0:T(8,128)S(1)}, f32[20,4096]{1,0:T(8,128)S(1)}, u32[]{:S(2)}, u32[]{:S(2)}) collective-permute-start(f32[20,4096]{1,0:T(8,128)S(1)} %broadcast_select_fusion.18), channel_id=1, source_target_pairs={{0,256},{16,272},{32,288},{48,304},{64,320},{80,336},{96,352},{112... | collective-permute-start | bytes 983048 | tf_op jit(solution)/shard_map/ppermute | solution.py:14
  123.2 17.4 %collective-permute-start.8 = (f32[20,4096]{1,0:T(8,128)}, f32[20,4096]{1,0:T(8,128)S(1)}, u32[]{:S(2)}, u32[]{:S(2)}) collective-permute-start(f32[20,4096]{1,0:T(8,128)} %broadcast_select_fusion.19), channel_id=1, source_target_pairs={{0,16},{16,0},{32,48},{48,32},{64,80},{80,64},{96,112},{112,96},{1... | collective-permute-start | bytes 983048 | tf_op jit(solution)/shard_map/ppermute | solution.py:20
  126.5 40.9 %collective-permute-start.10 = (f32[20,4096]{1,0:T(8,128)}, f32[20,4096]{1,0:T(8,128)}, u32[]{:S(2)}, u32[]{:S(2)}) collective-permute-start(f32[20,4096]{1,0:T(8,128)} %broadcast_select_fusion.19), channel_id=1, source_target_pairs={{0,480},{16,496},{32,0},{48,16},{64,32},{80,48},{96,64},{112,80},{... | collective-permute-start | bytes 983048 | tf_op jit(solution)/shard_map/ppermute | solution.py:14
  153.0 2.3 copy-start.3
  158.2 20.9 %copy-start.33 = (s32[24]{0:T(128)S(1)}, s32[24]{0:T(128)}, u32[]{:S(2)}) copy-start(s32[24]{0:T(128)} %get-tuple-element.62) | copy-start | bytes 292
  158.2 20.9 %copy-start.44 = (f32[24]{0:T(128)S(1)}, f32[24]{0:T(128)}, u32[]{:S(2)}) copy-start(f32[24]{0:T(128)} %compare_convert_fusion.7) | copy-start | bytes 292
  167.4 30.4 %collective-permute-start.11 = (f32[20,4096]{1,0:T(8,128)}, f32[20,4096]{1,0:T(8,128)}, u32[]{:S(2)}, u32[]{:S(2)}) collective-permute-start(f32[20,4096]{1,0:T(8,128)} %collective-permute-done.10), channel_id=1, source_target_pairs={{0,16},{16,0},{32,48},{48,32},{64,80},{80,64},{96,112},{112,96},{1... | collective-permute-start | bytes 983048 | tf_op jit(solution)/shard_map/ppermute | solution.py:20
  180.9 34.2 %collective-permute-start.13 = (f32[20,4096]{1,0:T(8,128)}, f32[20,4096]{1,0:T(8,128)}, u32[]{:S(2)}, u32[]{:S(2)}) collective-permute-start(f32[20,4096]{1,0:T(8,128)} %collective-permute-done.10), channel_id=1, source_target_pairs={{0,480},{16,496},{32,0},{48,16},{64,32},{80,48},{96,64},{112,80},{... | collective-permute-start | bytes 983048 | tf_op jit(solution)/shard_map/ppermute | solution.py:14
  212.1 5.0 %copy-start.12 = (f32[12,4096]{1,0:T(8,128)S(1)}, f32[12,4096]{1,0:T(8,128)}, u32[]{:S(2)}) copy-start(f32[12,4096]{1,0:T(8,128)} %convolution_add_fusion.6) | copy-start | bytes 589828
  212.1 5.0 %copy-start.29 = (s32[24]{0:T(128)S(1)}, s32[24]{0:T(128)}, u32[]{:S(2)}) copy-start(s32[24]{0:T(128)} %get-tuple-element.60) | copy-start | bytes 292
  212.1 5.1 %copy-start.42 = (f32[24]{0:T(128)S(1)}, f32[24]{0:T(128)}, u32[]{:S(2)}) copy-start(f32[24]{0:T(128)} %compare_convert_fusion.5) | copy-start | bytes 292
  215.1 3.1 %copy-start.5 = (f32[24,64,64]{2,1,0:T(8,128)S(1)}, f32[24,64,64]{2,1,0:T(8,128)}, u32[]{:S(2)}) copy-start(f32[24,64,64]{2,1,0:T(8,128)} %fusion.46) | copy-start | bytes 1179652
  215.1 22.7 %collective-permute-start.14 = (f32[20,4096]{1,0:T(8,128)}, f32[20,4096]{1,0:T(8,128)}, u32[]{:S(2)}, u32[]{:S(2)}) collective-permute-start(f32[20,4096]{1,0:T(8,128)} %collective-permute-done.13), channel_id=1, source_target_pairs={{0,16},{16,0},{32,48},{48,32},{64,80},{80,64},{96,112},{112,96},{1... | collective-permute-start | bytes 983048 | tf_op jit(solution)/shard_map/ppermute | solution.py:20
  218.6 34.8 %collective-permute-start.16 = (f32[20,4096]{1,0:T(8,128)}, f32[20,4096]{1,0:T(8,128)}, u32[]{:S(2)}, u32[]{:S(2)}) collective-permute-start(f32[20,4096]{1,0:T(8,128)} %collective-permute-done.13), channel_id=1, source_target_pairs={{0,480},{16,496},{32,0},{48,16},{64,32},{80,48},{96,64},{112,80},{... | collective-permute-start | bytes 983048 | tf_op jit(solution)/shard_map/ppermute | solution.py:14
  251.3 4.3 %copy-start.13 = (f32[12,4096]{1,0:T(8,128)S(1)}, f32[12,4096]{1,0:T(8,128)}, u32[]{:S(2)}) copy-start(f32[12,4096]{1,0:T(8,128)} %convolution_add_fusion.4) | copy-start | bytes 589828
  253.4 10.0 %collective-permute-start.17 = (f32[20,4096]{1,0:T(8,128)}, f32[20,4096]{1,0:T(8,128)}, u32[]{:S(2)}, u32[]{:S(2)}) collective-permute-start(f32[20,4096]{1,0:T(8,128)} %collective-permute-done.16), channel_id=1, source_target_pairs={{0,16},{16,0},{32,48},{48,32},{64,80},{80,64},{96,112},{112,96},{1... | collective-permute-start | bytes 983048 | tf_op jit(solution)/shard_map/ppermute | solution.py:20
  (32 other events, 36.8 us)
where the time goes:
time: 276 us; the launch traced here: 274 us
  starting transfers between devices  94.6 us (34%)
  waiting for transfers between devices  78.9 us (29%)
  local copies, waits for them, and re-layouts  49.1 us (18%)
  other arithmetic  25.8 us (9%)
  matrix products  25.2 us (9%)
    ppermute x14, starting transfers between devices, shifted_2(): lax.ppermute(shard, axis, [(i, (i + by) % devices) for i in range(devices)])  76.8 us
    ppermute x14, waiting for transfers between devices, shifted_2(): lax.ppermute(shard, axis, [(i, (i + by) % devices) for i in range(devices)])  44.5 us
    ppermute x4, waiting for transfers between devices, partner_2(): return lax.ppermute(value, axis, pairs)  34.5 us
    dot_general x8, matrix products, block_terms(): jnp.einsum('pik,pkj->pij', left_tiles, right_tiles, precision=lax.Precisi...  18.5 us
    ppermute x4, starting transfers between devices, partner_2(): return lax.ppermute(value, axis, pairs)  17.8 us
    gather x8, local copies, waits for them, and re-layouts, block_terms(): jnp.take(right_panel, right_index, axis=0)  10.5 us
    reshape x8, local copies, waits for them, and re-layouts, block_terms(): jnp.take(right_panel, right_index, axis=0)  10.1 us
    convert_element_type x8, other arithmetic, block_terms(): is_live = (jnp.arange(PRODUCTS) < live_count).astype(jnp.float32)  9.4 us
  transfers between devices with their start and end apart: 18, of which 9 were waited for; matrix products, arithmetic and copies ran while one was open for 31% of the time, Pallas kernels for 0%

commit v1 on v0

v1 whole, which is shorter than its diff:
```python
import functools

import jax
import jax.numpy as jnp
from jax import lax
from jax.experimental import pallas as pl
from jax.experimental.pallas import tpu as pltpu
from jax.sharding import PartitionSpec as P

TILE_SIDE = 64
LEFT_SLOTS = 4
RIGHT_SLOTS = 20
SINK_SLOTS = 12
PRODUCTS = 24
SECTIONS = 4
PANELS = 2 * SECTIONS
CHUNKS = 4
LEFT_ROWS = LEFT_SLOTS * TILE_SIDE
RIGHT_ROWS = RIGHT_SLOTS * TILE_SIDE // 2
CHUNK_ROWS = RIGHT_ROWS // CHUNKS
MESH = pl.DeviceIdType.MESH


def entry_offset(column):
    return column * 0 + 2


def exchange_kernel(rows, cols, left_ref, right_ref, left_all, right_all,
                    left_send, left_recv, entry_send, right_recv, down_send, up_send):
    row = lax.axis_index("row")
    column = lax.axis_index("col")
    parity = row % 2
    half_row = row // 2
    below = (row + rows - 1) % rows
    above = (row + 1) % rows
    offset = entry_offset(column)
    shift = (2 * column + offset) % rows
    entry_target = (row + rows - shift) % rows
    entry_source = (row + shift) % rows
    entry = parity + offset
    moves = shift != 0

    barrier = pltpu.get_barrier_semaphore()
    pl.semaphore_signal(barrier, inc=1, device_id=(below, column), device_id_type=MESH)
    pl.semaphore_signal(barrier, inc=1, device_id=(above, column), device_id_type=MESH)

    @pl.when(moves)
    def _():
        pl.semaphore_signal(barrier, inc=1, device_id=(entry_source, column), device_id_type=MESH)

    for section in range(SECTIONS):
        @pl.when((half_row + section) % cols != 0)
        def _():
            source = (column + half_row + section) % cols
            pl.semaphore_signal(barrier, inc=1, device_id=(row, source), device_id_type=MESH)

    peers = 2 + moves.astype(jnp.int32)
    for section in range(SECTIONS):
        peers += ((half_row + section) % cols != 0).astype(jnp.int32)
    pl.semaphore_wait(barrier, peers)

    def part(chunk):
        return pl.ds(pl.multiple_of(chunk * CHUNK_ROWS, 8), CHUNK_ROWS)

    def entry_copy(chunk):
        return pltpu.make_async_remote_copy(
            src_ref=right_ref.at[part(chunk)], dst_ref=right_all.at[entry, part(chunk)],
            send_sem=entry_send.at[chunk], recv_sem=right_recv.at[entry, chunk],
            device_id=(entry_target, column), device_id_type=MESH)

    def local_copy(chunk):
        return pltpu.make_async_copy(
            right_ref.at[part(chunk)], right_all.at[entry, part(chunk)], right_recv.at[entry, chunk])

    def left_copy(section):
        target = (column + 2 * cols - half_row - section) % cols
        return pltpu.make_async_remote_copy(
            src_ref=left_ref, dst_ref=left_all.at[section],
            send_sem=left_send.at[section], recv_sem=left_recv.at[section],
            device_id=(row, target), device_id_type=MESH)

    def left_local(section):
        return pltpu.make_async_copy(left_ref, left_all.at[section], left_recv.at[section])

    def down_copy(slot, chunk):
        return pltpu.make_async_remote_copy(
            src_ref=right_all.at[slot, part(chunk)],
            dst_ref=right_all.at[slot + 2 * (1 - parity), part(chunk)],
            send_sem=down_send.at[slot, chunk],
            recv_sem=right_recv.at[slot + 2 * (1 - parity), chunk],
            device_id=(below, column), device_id_type=MESH)

    def up_copy(slot, chunk):
        return pltpu.make_async_remote_copy(
            src_ref=right_all.at[slot, part(chunk)],
            dst_ref=right_all.at[slot - 2 * parity, part(chunk)],
            send_sem=up_send.at[slot, chunk],
            recv_sem=right_recv.at[slot - 2 * parity, chunk],
            device_id=(above, column), device_id_type=MESH)

    for chunk in range(CHUNKS):
        @pl.when(moves)
        def _():
            entry_copy(chunk).start()

        @pl.when(jnp.logical_not(moves))
        def _():
            local_copy(chunk).start()

    for section in range(SECTIONS):
        @pl.when((half_row + section) % cols != 0)
        def _():
            left_copy(section).start()

        @pl.when((half_row + section) % cols == 0)
        def _():
            left_local(section).start()

    last_down = PANELS - 1 - 2 * (1 - parity)
    last_up = 2 * parity

    def arrived(slot, chunk):
        pltpu.make_async_copy(
            right_ref.at[part(chunk)], right_all.at[slot, part(chunk)], right_recv.at[slot, chunk]).wait()

    def first(chunk, carry):
        arrived(entry, chunk)

        @pl.when(entry <= last_down)
        def _():
            down_copy(entry, chunk).start()

        @pl.when(entry >= last_up)
        def _():
            up_copy(entry, chunk).start()
        return carry

    lax.fori_loop(0, CHUNKS, first, 0)

    def onward(step, carry):
        distance = step // CHUNKS + 1
        chunk = step % CHUNKS
        higher = entry + distance
        lower = entry - distance

        @pl.when(higher < PANELS)
        def _():
            arrived(higher, chunk)

        @pl.when(higher <= last_down)
        def _():
            down_copy(higher, chunk).start()

        @pl.when(lower >= 0)
        def _():
            arrived(lower, chunk)

        @pl.when(lower >= last_up)
        def _():
            up_copy(lower, chunk).start()
        return carry

    lax.fori_loop(0, (PANELS - 1) * CHUNKS, onward, 0)

    def sent(step, carry):
        slot = step // CHUNKS
        chunk = step % CHUNKS

        @pl.when((slot >= entry) & (slot <= last_down))
        def _():
            down_copy(slot, chunk).wait_send()

        @pl.when((slot <= entry) & (slot >= last_up))
        def _():
            up_copy(slot, chunk).wait_send()
        return carry

    lax.fori_loop(0, PANELS * CHUNKS, sent, 0)

    for chunk in range(CHUNKS):
        @pl.when(moves)
        def _():
            entry_copy(chunk).wait_send()

    for section in range(SECTIONS):
        @pl.when((half_row + section) % cols != 0)
        def _():
            left_copy(section).wait()

        @pl.when((half_row + section) % cols == 0)
        def _():
            left_local(section).wait()


def exchange(rows, cols, left, right):
    dma = pltpu.SemaphoreType.DMA
    return pl.pallas_call(
        functools.partial(exchange_kernel, rows, cols),
        out_shape=(
            jax.ShapeDtypeStruct((SECTIONS, LEFT_ROWS, 2 * TILE_SIDE), jnp.float32),
            jax.ShapeDtypeStruct((PANELS, RIGHT_ROWS, 2 * TILE_SIDE), jnp.float32),
        ),
        in_specs=[pl.BlockSpec(memory_space=pltpu.VMEM)] * 2,
        out_specs=(pl.BlockSpec(memory_space=pltpu.VMEM),) * 2,
        scratch_shapes=[
            dma((SECTIONS,)), dma((SECTIONS,)), dma((CHUNKS,)), dma((PANELS, CHUNKS)),
            dma((PANELS, CHUNKS)), dma((PANELS, CHUNKS)),
        ],
        compiler_params=pltpu.CompilerParams(collective_id=0, has_side_effects=True),
        name="exchange",
    )(left, right)


def product_kernel(left_lists, right_lists, sink_lists, counts, left_all, right_all, out, products, sums):
    side = TILE_SIDE
    sums[...] = jnp.zeros_like(sums)
    lane = lax.broadcasted_iota(jnp.int32, (LEFT_ROWS, 2 * side), 1)

    def section_body(section, carry):
        left = left_all[section]
        turned = pltpu.roll(left, side, 1)
        for half in range(2):
            own, other = (left, turned) if half == 0 else (turned, left)
            twice = jnp.where(lane < side, own, other)
            high = twice.astype(jnp.bfloat16).astype(jnp.float32)
            split = jnp.where(lane < side, high, twice - high).astype(jnp.bfloat16)
            stream = jnp.concatenate([split, split], axis=1)
            item = 2 * section + half
            for quad in range(RIGHT_SLOTS // 4):
                right = jnp.concatenate(
                    [right_all[item, pl.ds((2 * quad + n) * side, side), :] for n in range(2)], axis=1)
                right_high = right.astype(jnp.bfloat16)
                right_low = (right - right_high.astype(jnp.float32)).astype(jnp.bfloat16)
                held = jnp.concatenate([right_high, right_high, right_low, right_low], axis=0)
                found = jnp.dot(stream, held, preferred_element_type=jnp.float32)
                for n in range(2):
                    products[pl.ds(LEFT_SLOTS * (2 * quad + n), LEFT_SLOTS)] = (
                        found[:, 2 * side * n : 2 * side * (n + 1)].reshape(LEFT_SLOTS, side, 2 * side))

            def add(position, inner):
                right_slot = right_lists[item, position]
                source = LEFT_SLOTS * (right_slot >> 1) + left_lists[item, position]
                sink = 2 * sink_lists[item, position] + (right_slot & 1)
                sums[sink] += products[source]
                return inner

            lax.fori_loop(0, counts[item], add, 0)
        return carry

    lax.fori_loop(0, SECTIONS, section_body, 0)
    for sink in range(SINK_SLOTS):
        total = sums[2 * sink] + pltpu.roll(sums[2 * sink + 1], side, 1)
        out[sink] = total[:, :side]


def product_sums(left_lists, right_lists, sink_lists, counts, left_all, right_all):
    smem = pl.BlockSpec(memory_space=pltpu.SMEM)
    vmem = pl.BlockSpec(memory_space=pltpu.VMEM)
    return pl.pallas_call(
        product_kernel,
        out_shape=jax.ShapeDtypeStruct((SINK_SLOTS, TILE_SIDE, TILE_SIDE), jnp.float32),
        in_specs=[smem] * 4 + [vmem] * 2,
        out_specs=vmem,
        scratch_shapes=[
            pltpu.VMEM((LEFT_SLOTS * RIGHT_SLOTS // 2, TILE_SIDE, 2 * TILE_SIDE), jnp.float32),
            pltpu.VMEM((2 * SINK_SLOTS, TILE_SIDE, 2 * TILE_SIDE), jnp.float32),
        ],
        name="product_sums",
    )(left_lists, right_lists, sink_lists, counts, left_all, right_all)


def per_device(rows, cols, left_blocks, right_blocks, left_slots, right_slots, sink_slots, live_counts):
    side = TILE_SIDE
    right = right_blocks.reshape(RIGHT_SLOTS // 2, 2, side, side).transpose(0, 2, 1, 3).reshape(RIGHT_ROWS, 2 * side)
    left = left_blocks.reshape(2, LEFT_ROWS, side).transpose(1, 0, 2).reshape(LEFT_ROWS, 2 * side)
    left_all, right_all = exchange(rows, cols, left, right)
    total = product_sums(
        left_slots.reshape(PANELS, PRODUCTS), right_slots.reshape(PANELS, PRODUCTS),
        sink_slots.reshape(PANELS, PRODUCTS), live_counts.reshape(PANELS), left_all, right_all)
    return total.reshape(1, 1, SINK_SLOTS, side * side)


def solution(mesh):
    return jax.shard_map(
        functools.partial(per_device, mesh.shape["row"], mesh.shape["col"]),
        mesh=mesh,
        in_specs=(
            P("row", "col", None, None),
            P("row", "col", None, None),
            P("row", "col", None, None, None),
            P("row", "col", None, None, None),
            P("row", "col", None, None, None),
            P("row", "col", None, None),
        ),
        out_specs=P("row", "col", None, None),
        check_vma=False,
    )
```

time: 276 us -> 105 us (0.38)
  the two profiles are of different devices: /device:TPU:146 before, /device:TPU:9 now
where the time goes in v1:
time: 105 us
  Pallas kernels  97.4 us (93%)
  local copies, waits for them, and re-layouts  5.51 us (5%)
  other arithmetic  1.81 us (2%)
    pallas_call x1, Pallas kernels, exchange(): pl.pallas_call(functools.partial(exchange_kernel, rows, cols), out_shape=...  90.3 us
    pallas_call x1, Pallas kernels, product_sums(): pl.pallas_call(product_kernel, out_shape=jax.ShapeDtypeStruct((SINK_SLOTS...  7.06 us

profile of v1, /device:TPU:9, one launch (start us, length us, event | category | flops | bytes accessed | tf_op | source)
XLA Modules:
  0.0 104.7 jit_solution(1391991183081729645)
XLA Ops:
  0.0 0.0 copy-start
  0.0 0.0 copy-start.1
  0.0 1.8 %reduce = f32[20,4096]{1,0:T(8,128)S(1)} reduce(f32[1,1,20,4096]{3,1,2,0:T(1,128)} %param.7, f32[]{:T(128)} %constant.6), dimensions={0,1}, to_apply=%param.7.reduce_sub_computation | reduce | bytes 655364 | tf_op args[1]
  1.8 0.2 reshape.33
  2.1 0.5 copy.17
  2.6 1.1 %reshape.34.right_ref = f32[640,128]{1,0:T(8,128)} reshape(f32[10,64,2,64]{3,2,1,0:T(2,128)S(1)} %bitcast.8) | data formatting | bytes 655360 | tf_op jit(solution)/shard_map/reshape | solution.py:274
  3.7 0.0 copy-done
  3.7 0.2 reshape.31
  3.9 0.1 copy.12
  4.0 0.8 copy.14.left_ref
  4.8 90.3 %exchange.1 = (f32[4,256,128]{2,1,0:T(8,128)}, f32[8,640,128]{2,1,0:T(8,128)}) custom-call(f32[256,128]{1,0:T(8,128)} %copy.14.left_ref, f32[640,128]{1,0:T(8,128)} %reshape.34.right_ref), custom_call_target="tpu_custom_call" | custom-call | tf_op jit(solution)/shard_map/exchange/pallas_call | solution.py:197
  95.1 0.0 copy-done.1
  95.1 0.1 copy.11
  95.2 0.6 reshape.30.counts
  95.8 7.1 %product_sums.1 = f32[12,64,64]{2,1,0:T(8,128)} custom-call(s32[8,24]{1,0:T(8,128)} %bitcast.11, s32[8,24]{1,0:T(8,128)} %bitcast.12, s32[8,24]{1,0:T(8,128)} %bitcast.13, s32[8]{0:T(128)} %reshape.30.counts, f32[4,256,128]{2,1,0:T(8,128)} %get-tuple-element.7.left_all, f32[8,640,128]{2,1,0:T(8,128)} %get-tuple-element.8.right_all), custom_call_target="tpu_custom_call" | custom-call | tf_op jit(solution)/shard_map/product_sums/pallas_call | solution.py:259
  102.8 1.9 %reshape.36 = f32[1,1,12,4096]{3,1,2,0:T(1,128)} reshape(f32[12,64,64]{2,1,0:T(8,128)} %product_sums.1) | data formatting | bytes 393216 | tf_op jit(solution)/shard_map/reshape | solution.py:280
Async XLA Ops:
  0.0 3.7 %copy-start = (f32[1,2,4,4096]{3,2,1,0:T(4,128)S(1)}, f32[1,2,4,4096]{3,2,1,0:T(4,128)}, u32[]{:S(2)}) copy-start(f32[1,2,4,4096]{3,2,1,0:T(4,128)} %param.6) | copy-start | bytes 393220
  0.0 95.1 %copy-start.1 = (s32[1,1,4,2]{2,3,1,0:T(2,128)S(1)}, s32[1,1,4,2]{2,3,1,0:T(2,128)}, u32[]{:S(2)}) copy-start(s32[1,1,4,2]{2,3,1,0:T(2,128)} %param.11) | copy-start | bytes 100

commit v2 on v1

--- a/solution.py
+++ b/solution.py
@@ -18,59 +18,95 @@
 LEFT_ROWS = LEFT_SLOTS * TILE_SIDE
 RIGHT_ROWS = RIGHT_SLOTS * TILE_SIDE // 2
 CHUNK_ROWS = RIGHT_ROWS // CHUNKS
+TURNED = CHUNKS // 2
 MESH = pl.DeviceIdType.MESH
 
 
-def entry_offset(column):
-    return column * 0 + 2
-
-
-def exchange_kernel(rows, cols, left_ref, right_ref, left_all, right_all,
-                    left_send, left_recv, entry_send, right_recv, down_send, up_send):
+def chosen(column, values):
+    total = 0
+    for place, value in enumerate(values):
+        if value:
+            total = total + (column % len(values) == place).astype(jnp.int32) * value
+    return total
+
+
+def exchange_kernel(rows, cols, left_ref, right_ref, left_all, right_all, relay,
+                    left_send, left_recv, entry_send, right_recv, down_send, up_send,
+                    relay_send, relay_recv):
     row = lax.axis_index("row")
     column = lax.axis_index("col")
     parity = row % 2
     half_row = row // 2
     below = (row + rows - 1) % rows
     above = (row + 1) % rows
-    offset = entry_offset(column)
+    offset = chosen(column, (0, 0, 0, 6, 6, 6, 4, 2))
+    turned_offset = chosen(column, (0, 6, 0, 6, 0, 6, 4, 2))
+    relay_shift = chosen(column, (0, rows - 4, 0, 0, 4, 0, 0, 0))
+    relays = relay_shift != 0
     shift = (2 * column + offset) % rows
-    entry_target = (row + rows - shift) % rows
-    entry_source = (row + shift) % rows
-    entry = parity + offset
+    final_shift = (2 * column + turned_offset + rows - relay_shift) % rows
     moves = shift != 0
+    greets_final = relays & (final_shift != relay_shift)
+
+    def greet(row_to, column_to):
+        pl.semaphore_signal(barrier, inc=1, device_id=(row_to, column_to), device_id_type=MESH)
 
     barrier = pltpu.get_barrier_semaphore()
-    pl.semaphore_signal(barrier, inc=1, device_id=(below, column), device_id_type=MESH)
-    pl.semaphore_signal(barrier, inc=1, device_id=(above, column), device_id_type=MESH)
+    greet(below, column)
+    greet(above, column)
 
     @pl.when(moves)
     def _():
-        pl.semaphore_signal(barrier, inc=1, device_id=(entry_source, column), device_id_type=MESH)
+        greet((row + shift) % rows, column)
+
+    @pl.when(relays)
+    def _():
+        greet((row + relay_shift) % rows, column)
+
+    @pl.when(greets_final)
+    def _():
+        greet((row + final_shift) % rows, column)
 
     for section in range(SECTIONS):
         @pl.when((half_row + section) % cols != 0)
         def _():
-            source = (column + half_row + section) % cols
-            pl.semaphore_signal(barrier, inc=1, device_id=(row, source), device_id_type=MESH)
-
-    peers = 2 + moves.astype(jnp.int32)
+            greet(row, (column + half_row + section) % cols)
+
+    peers = 2 + moves.astype(jnp.int32) + relays.astype(jnp.int32) + greets_final.astype(jnp.int32)
     for section in range(SECTIONS):
         peers += ((half_row + section) % cols != 0).astype(jnp.int32)
     pl.semaphore_wait(barrier, peers)
 
+    def entry_of(chunk):
+        if isinstance(chunk, int):
+            return parity + (turned_offset if chunk < TURNED else offset)
+        return parity + offset + (chunk < TURNED).astype(jnp.int32) * (turned_offset - offset)
+
     def part(chunk):
         return pl.ds(pl.multiple_of(chunk * CHUNK_ROWS, 8), CHUNK_ROWS)
 
     def entry_copy(chunk):
         return pltpu.make_async_remote_copy(
-            src_ref=right_ref.at[part(chunk)], dst_ref=right_all.at[entry, part(chunk)],
-            send_sem=entry_send.at[chunk], recv_sem=right_recv.at[entry, chunk],
-            device_id=(entry_target, column), device_id_type=MESH)
+            src_ref=right_ref.at[part(chunk)], dst_ref=right_all.at[entry_of(chunk), part(chunk)],
+            send_sem=entry_send.at[chunk], recv_sem=right_recv.at[entry_of(chunk), chunk],
+            device_id=((row + rows - shift) % rows, column), device_id_type=MESH)
 
     def local_copy(chunk):
         return pltpu.make_async_copy(
-            right_ref.at[part(chunk)], right_all.at[entry, part(chunk)], right_recv.at[entry, chunk])
+            right_ref.at[part(chunk)], right_all.at[entry_of(chunk), part(chunk)],
+            right_recv.at[entry_of(chunk), chunk])
+
+    def relay_copy(chunk):
+        return pltpu.make_async_remote_copy(
+            src_ref=right_ref.at[part(chunk)], dst_ref=relay.at[part(chunk)],
+            send_sem=entry_send.at[chunk], recv_sem=relay_recv.at[chunk],
+            device_id=((row + rows - relay_shift) % rows, column), device_id_type=MESH)
+
+    def final_copy(chunk):
+        return pltpu.make_async_remote_copy(
+            src_ref=relay.at[part(chunk)], dst_ref=right_all.at[entry_of(chunk), part(chunk)],
+            send_sem=relay_send.at[chunk], recv_sem=right_recv.at[entry_of(chunk), chunk],
+            device_id=((row + rows - final_shift) % rows, column), device_id_type=MESH)
 
     def left_copy(section):
         target = (column + 2 * cols - half_row - section) % cols
@@ -99,13 +135,20 @@
             device_id=(above, column), device_id_type=MESH)
 
     for chunk in range(CHUNKS):
-        @pl.when(moves)
+        direct = moves if chunk >= TURNED else moves & jnp.logical_not(relays)
+
+        @pl.when(direct)
         def _():
             entry_copy(chunk).start()
 
         @pl.when(jnp.logical_not(moves))
         def _():
             local_copy(chunk).start()
+
+        if chunk < TURNED:
+            @pl.when(relays)
+            def _():
+                relay_copy(chunk).start()
 
     for section in range(SECTIONS):
         @pl.when((half_row + section) % cols != 0)
@@ -124,6 +167,7 @@
             right_ref.at[part(chunk)], right_all.at[slot, part(chunk)], right_recv.at[slot, chunk]).wait()
 
     def first(chunk, carry):
+        entry = entry_of(chunk)
         arrived(entry, chunk)
 
         @pl.when(entry <= last_down)
@@ -135,13 +179,21 @@
             up_copy(entry, chunk).start()
         return carry
 
-    lax.fori_loop(0, CHUNKS, first, 0)
+    lax.fori_loop(TURNED, CHUNKS, first, 0)
+
+    @pl.when(relays)
+    def _():
+        for chunk in range(TURNED):
+            relay_copy(chunk).wait_recv()
+            final_copy(chunk).start()
+
+    lax.fori_loop(0, TURNED, first, 0)
 
     def onward(step, carry):
         distance = step // CHUNKS + 1
-        chunk = step % CHUNKS
-        higher = entry + distance
-        lower = entry - distance
+        chunk = (step + TURNED) % CHUNKS
+        higher = entry_of(chunk) + distance
+        lower = entry_of(chunk) - distance
 
         @pl.when(higher < PANELS)
         def _():
@@ -165,6 +217,7 @@
     def sent(step, carry):
         slot = step // CHUNKS
         chunk = step % CHUNKS
+        entry = entry_of(chunk)
 
         @pl.when((slot >= entry) & (slot <= last_down))
         def _():
@@ -181,6 +234,11 @@
         @pl.when(moves)
         def _():
             entry_copy(chunk).wait_send()
+
+        if chunk < TURNED:
+            @pl.when(relays)
+            def _():
+                final_copy(chunk).wait_send()
 
     for section in range(SECTIONS):
         @pl.when((half_row + section) % cols != 0)
@@ -203,8 +261,9 @@
         in_specs=[pl.BlockSpec(memory_space=pltpu.VMEM)] * 2,
         out_specs=(pl.BlockSpec(memory_space=pltpu.VMEM),) * 2,
         scratch_shapes=[
+            pltpu.VMEM((TURNED * CHUNK_ROWS, 2 * TILE_SIDE), jnp.float32),
             dma((SECTIONS,)), dma((SECTIONS,)), dma((CHUNKS,)), dma((PANELS, CHUNKS)),
-            dma((PANELS, CHUNKS)), dma((PANELS, CHUNKS)),
+            dma((PANELS, CHUNKS)), dma((PANELS, CHUNKS)), dma((TURNED,)), dma((TURNED,)),
         ],
         compiler_params=pltpu.CompilerParams(collective_id=0, has_side_effects=True),
         name="exchange",

time: 105 us -> 84.2 us (0.80)
  the two profiles are of different devices: /device:TPU:9 before, /device:TPU:2 now
where the time goes in v2:
time: 84.2 us; the launch traced here: 84 us
  Pallas kernels  76.6 us (91%)
  local copies, waits for them, and re-layouts  5.51 us (7%)
  other arithmetic  1.81 us (2%)
    pallas_call x1, Pallas kernels, exchange(): pl.pallas_call(functools.partial(exchange_kernel, rows, cols), out_shape=...  69.8 us
    pallas_call x1, Pallas kernels, product_sums(): pl.pallas_call(product_kernel, out_shape=jax.ShapeDtypeStruct((SINK_SLOTS...  6.76 us
    reshape x1, local copies, waits for them, and re-layouts, per_device(): return total.reshape(1, 1, SINK_SLOTS, side * side)  1.91 us
    reshape x3, local copies, waits for them, and re-layouts, per_device(): right_blocks.reshape(RIGHT_SLOTS // 2, 2, side, side).transpose(0, 2, 1, 3)  1.85 us
    unnamed x1, other arithmetic  1.81 us

profile of v2, /device:TPU:2, one launch (start us, length us, event | category | flops | bytes accessed | tf_op | source)
XLA Modules:
  0.0 84.0 jit_solution(1896392997299359871)
XLA Ops:
  0.0 0.0 copy-start
  0.0 0.0 copy-start.1
  0.0 1.8 %reduce = f32[20,4096]{1,0:T(8,128)S(1)} reduce(f32[1,1,20,4096]{3,1,2,0:T(1,128)} %param.7, f32[]{:T(128)} %constant.6), dimensions={0,1}, to_apply=%param.7.reduce_sub_computation | reduce | bytes 655364 | tf_op args[1]
  1.8 0.2 reshape.33
  2.1 0.5 copy.17
  2.6 1.1 %reshape.34.right_ref = f32[640,128]{1,0:T(8,128)} reshape(f32[10,64,2,64]{3,2,1,0:T(2,128)S(1)} %bitcast.8) | data formatting | bytes 655360 | tf_op jit(solution)/shard_map/reshape | solution.py:333
  3.7 0.0 copy-done
  3.7 0.2 reshape.31
  3.9 0.1 copy.12
  4.0 0.8 copy.14.left_ref
  4.8 69.8 %exchange.1 = (f32[4,256,128]{2,1,0:T(8,128)}, f32[8,640,128]{2,1,0:T(8,128)}) custom-call(f32[256,128]{1,0:T(8,128)} %copy.14.left_ref, f32[640,128]{1,0:T(8,128)} %reshape.34.right_ref), custom_call_target="tpu_custom_call" | custom-call | tf_op jit(solution)/shard_map/exchange/pallas_call | solution.py:255
  74.6 0.0 copy-done.1
  74.6 0.1 copy.11
  74.7 0.6 reshape.30.counts
  75.3 6.8 %product_sums.1 = f32[12,64,64]{2,1,0:T(8,128)} custom-call(s32[8,24]{1,0:T(8,128)} %bitcast.11, s32[8,24]{1,0:T(8,128)} %bitcast.12, s32[8,24]{1,0:T(8,128)} %bitcast.13, s32[8]{0:T(128)} %reshape.30.counts, f32[4,256,128]{2,1,0:T(8,128)} %get-tuple-element.7.left_all, f32[8,640,128]{2,1,0:T(8,128)} %get-tuple-element.8.right_all), custom_call_target="tpu_custom_call" | custom-call | tf_op jit(solution)/shard_map/product_sums/pallas_call | solution.py:318
  82.0 1.9 %reshape.36 = f32[1,1,12,4096]{3,1,2,0:T(1,128)} reshape(f32[12,64,64]{2,1,0:T(8,128)} %product_sums.1) | data formatting | bytes 393216 | tf_op jit(solution)/shard_map/reshape | solution.py:339
Async XLA Ops:
  0.0 3.7 %copy-start = (f32[1,2,4,4096]{3,2,1,0:T(4,128)S(1)}, f32[1,2,4,4096]{3,2,1,0:T(4,128)}, u32[]{:S(2)}) copy-start(f32[1,2,4,4096]{3,2,1,0:T(4,128)} %param.6) | copy-start | bytes 393220
  0.0 74.6 %copy-start.1 = (s32[1,1,4,2]{2,3,1,0:T(2,128)S(1)}, s32[1,1,4,2]{2,3,1,0:T(2,128)}, u32[]{:S(2)}) copy-start(s32[1,1,4,2]{2,3,1,0:T(2,128)} %param.11) | copy-start | bytes 100

commit v3 on v2

--- a/solution.py
+++ b/solution.py
@@ -14,11 +14,12 @@
 PRODUCTS = 24
 SECTIONS = 4
 PANELS = 2 * SECTIONS
-CHUNKS = 4
+CHUNKS = 8
 LEFT_ROWS = LEFT_SLOTS * TILE_SIDE
 RIGHT_ROWS = RIGHT_SLOTS * TILE_SIDE // 2
 CHUNK_ROWS = RIGHT_ROWS // CHUNKS
-TURNED = CHUNKS // 2
+TURNED = 5
+LAG = 2
 MESH = pl.DeviceIdType.MESH
 
 
@@ -187,32 +188,34 @@
             relay_copy(chunk).wait_recv()
             final_copy(chunk).start()
 
-    lax.fori_loop(0, TURNED, first, 0)
+    lag = LAG * relays.astype(jnp.int32)
 
     def onward(step, carry):
-        distance = step // CHUNKS + 1
         chunk = (step + TURNED) % CHUNKS
+        turned = chunk < TURNED
+        distance = step // CHUNKS - lag * turned.astype(jnp.int32)
+        begun = (distance > 0) | (turned & (distance == 0))
         higher = entry_of(chunk) + distance
         lower = entry_of(chunk) - distance
 
-        @pl.when(higher < PANELS)
+        @pl.when(begun & (higher < PANELS))
         def _():
             arrived(higher, chunk)
 
-        @pl.when(higher <= last_down)
+        @pl.when(begun & (higher <= last_down))
         def _():
             down_copy(higher, chunk).start()
 
-        @pl.when(lower >= 0)
+        @pl.when((distance > 0) & (lower >= 0))
         def _():
             arrived(lower, chunk)
 
-        @pl.when(lower >= last_up)
+        @pl.when(begun & (lower >= last_up))
         def _():
             up_copy(lower, chunk).start()
         return carry
 
-    lax.fori_loop(0, (PANELS - 1) * CHUNKS, onward, 0)
+    lax.fori_loop(0, (PANELS + LAG) * CHUNKS, onward, 0)
 
     def sent(step, carry):
         slot = step // CHUNKS

time: 84.2 us -> 86.8 us (1.031)
  Pallas kernels: 76.6 us -> 79.3 us
    pallas_call x1, Pallas kernels: 69.8 us -> 72.2 us  [exchange(): pl.pallas_call(functools.partial(exchange_kernel, rows, cols), out_shape=...]
where the time goes in v3:
time: 86.8 us; the launch traced here: 86.6 us
  Pallas kernels  79.3 us (91%)
  local copies, waits for them, and re-layouts  5.51 us (6%)
  other arithmetic  1.81 us (2%)
    pallas_call x1, Pallas kernels, exchange(): pl.pallas_call(functools.partial(exchange_kernel, rows, cols), out_shape=...  72.2 us
    pallas_call x1, Pallas kernels, product_sums(): pl.pallas_call(product_kernel, out_shape=jax.ShapeDtypeStruct((SINK_SLOTS...  7.05 us
    reshape x1, local copies, waits for them, and re-layouts, per_device(): return total.reshape(1, 1, SINK_SLOTS, side * side)  1.91 us
    reshape x3, local copies, waits for them, and re-layouts, per_device(): right_blocks.reshape(RIGHT_SLOTS // 2, 2, side, side).transpose(0, 2, 1, 3)  1.85 us
    unnamed x1, other arithmetic  1.81 us

profile of v3, /device:TPU:2, one launch (start us, length us, event | category | flops | bytes accessed | tf_op | source)
XLA Modules:
  0.0 86.6 jit_solution(5703923259461416581)
XLA Ops:
  0.0 0.0 copy-start
  0.0 0.0 copy-start.1
  0.0 1.8 %reduce = f32[20,4096]{1,0:T(8,128)S(1)} reduce(f32[1,1,20,4096]{3,1,2,0:T(1,128)} %param.7, f32[]{:T(128)} %constant.6), dimensions={0,1}, to_apply=%param.7.reduce_sub_computation | reduce | bytes 655364 | tf_op args[1]
  1.8 0.2 reshape.33
  2.1 0.5 copy.17
  2.6 1.1 %reshape.34.right_ref = f32[640,128]{1,0:T(8,128)} reshape(f32[10,64,2,64]{3,2,1,0:T(2,128)S(1)} %bitcast.8) | data formatting | bytes 655360 | tf_op jit(solution)/shard_map/reshape | solution.py:336
  3.7 0.0 copy-done
  3.7 0.2 reshape.31
  3.9 0.1 copy.12
  4.0 0.8 copy.14.left_ref
  4.8 72.2 %exchange.1 = (f32[4,256,128]{2,1,0:T(8,128)}, f32[8,640,128]{2,1,0:T(8,128)}) custom-call(f32[256,128]{1,0:T(8,128)} %copy.14.left_ref, f32[640,128]{1,0:T(8,128)} %reshape.34.right_ref), custom_call_target="tpu_custom_call" | custom-call | tf_op jit(solution)/shard_map/exchange/pallas_call | solution.py:258
  77.0 0.0 copy-done.1
  77.0 0.1 copy.11
  77.1 0.6 reshape.30.counts
  77.7 7.0 %product_sums.1 = f32[12,64,64]{2,1,0:T(8,128)} custom-call(s32[8,24]{1,0:T(8,128)} %bitcast.11, s32[8,24]{1,0:T(8,128)} %bitcast.12, s32[8,24]{1,0:T(8,128)} %bitcast.13, s32[8]{0:T(128)} %reshape.30.counts, f32[4,256,128]{2,1,0:T(8,128)} %get-tuple-element.7.left_all, f32[8,640,128]{2,1,0:T(8,128)} %get-tuple-element.8.right_all), custom_call_target="tpu_custom_call" | custom-call | tf_op jit(solution)/shard_map/product_sums/pallas_call | solution.py:321
  84.7 1.9 %reshape.36 = f32[1,1,12,4096]{3,1,2,0:T(1,128)} reshape(f32[12,64,64]{2,1,0:T(8,128)} %product_sums.1) | data formatting | bytes 393216 | tf_op jit(solution)/shard_map/reshape | solution.py:342
Async XLA Ops:
  0.0 3.7 %copy-start = (f32[1,2,4,4096]{3,2,1,0:T(4,128)S(1)}, f32[1,2,4,4096]{3,2,1,0:T(4,128)}, u32[]{:S(2)}) copy-start(f32[1,2,4,4096]{3,2,1,0:T(4,128)} %param.6) | copy-start | bytes 393220
  0.0 77.0 %copy-start.1 = (s32[1,1,4,2]{2,3,1,0:T(2,128)S(1)}, s32[1,1,4,2]{2,3,1,0:T(2,128)}, u32[]{:S(2)}) copy-start(s32[1,1,4,2]{2,3,1,0:T(2,128)} %param.11) | copy-start | bytes 100

commit v4 on v2

--- a/solution.py
+++ b/solution.py
@@ -272,54 +272,78 @@
 
 def product_kernel(left_lists, right_lists, sink_lists, counts, left_all, right_all, out, products, sums):
     side = TILE_SIDE
-    sums[...] = jnp.zeros_like(sums)
-    lane = lax.broadcasted_iota(jnp.int32, (LEFT_ROWS, 2 * side), 1)
-
-    def section_body(section, carry):
-        left = left_all[section]
+    section = pl.program_id(0)
+
+    @pl.when(section == 0)
+    def _():
+        sums[...] = jnp.zeros_like(sums)
+
+    def ordered(count):
+        return lax.broadcasted_iota(jnp.int32, (count, 2 * side), 1) < side
+
+    place = lax.broadcasted_iota(jnp.int32, (2 * side, 2 * side), 0)
+    target = lax.broadcasted_iota(jnp.int32, (2 * side, 2 * side), 1)
+    moved = (place & side) + (place & 1) * (side // 2) + ((place & (side - 1)) >> 1)
+    evens_first = (moved == target).astype(jnp.float32).astype(jnp.bfloat16)
+    rows = LEFT_ROWS // 2
+    low_lanes, low_lanes_left = ordered(side // 2), ordered(rows)
+    for half in range(2):
+        left = left_all[0, pl.ds(half * rows, rows), :]
         turned = pltpu.roll(left, side, 1)
-        for half in range(2):
-            own, other = (left, turned) if half == 0 else (turned, left)
-            twice = jnp.where(lane < side, own, other)
-            high = twice.astype(jnp.bfloat16).astype(jnp.float32)
-            split = jnp.where(lane < side, high, twice - high).astype(jnp.bfloat16)
-            stream = jnp.concatenate([split, split], axis=1)
-            item = 2 * section + half
-            for quad in range(RIGHT_SLOTS // 4):
-                right = jnp.concatenate(
-                    [right_all[item, pl.ds((2 * quad + n) * side, side), :] for n in range(2)], axis=1)
-                right_high = right.astype(jnp.bfloat16)
-                right_low = (right - right_high.astype(jnp.float32)).astype(jnp.bfloat16)
-                held = jnp.concatenate([right_high, right_high, right_low, right_low], axis=0)
-                found = jnp.dot(stream, held, preferred_element_type=jnp.float32)
-                for n in range(2):
-                    products[pl.ds(LEFT_SLOTS * (2 * quad + n), LEFT_SLOTS)] = (
-                        found[:, 2 * side * n : 2 * side * (n + 1)].reshape(LEFT_SLOTS, side, 2 * side))
-
-            def add(position, inner):
-                right_slot = right_lists[item, position]
-                source = LEFT_SLOTS * (right_slot >> 1) + left_lists[item, position]
-                sink = 2 * sink_lists[item, position] + (right_slot & 1)
-                sums[sink] += products[source]
-                return inner
-
-            lax.fori_loop(0, counts[item], add, 0)
-        return carry
-
-    lax.fori_loop(0, SECTIONS, section_body, 0)
-    for sink in range(SINK_SLOTS):
-        total = sums[2 * sink] + pltpu.roll(sums[2 * sink + 1], side, 1)
-        out[sink] = total[:, :side]
+        even = jnp.where(low_lanes_left, left, turned).reshape(LEFT_SLOTS, side // 2, 2 * side)
+        odd = jnp.where(low_lanes_left, turned, left).reshape(LEFT_SLOTS, side // 2, 2 * side)
+        twice = jnp.concatenate([even, odd], axis=1).reshape(LEFT_ROWS, 2 * side)
+        high = twice.astype(jnp.bfloat16).astype(jnp.float32)
+        split = jnp.where(ordered(LEFT_ROWS), high, twice - high).astype(jnp.bfloat16)
+        split = jnp.dot(split, evens_first, preferred_element_type=jnp.float32).astype(jnp.bfloat16)
+        stream = jnp.concatenate([split, split], axis=1)
+        item = 2 * section + half
+        for quad in range(RIGHT_SLOTS // 4):
+            pairs = []
+            for pair in range(2):
+                base = (4 * quad + 2 * pair) * (side // 2)
+                first = right_all[half, pl.ds(base, side // 2), :]
+                second = right_all[half, pl.ds(base + side // 2, side // 2), :]
+                pairs.append(jnp.concatenate([
+                    jnp.where(low_lanes, first, pltpu.roll(second, side, 1)),
+                    jnp.where(low_lanes, pltpu.roll(first, side, 1), second)], axis=0))
+            right = jnp.concatenate(pairs, axis=1)
+            right_high = right.astype(jnp.bfloat16)
+            right_low = (right - right_high.astype(jnp.float32)).astype(jnp.bfloat16)
+            held = jnp.concatenate([right_high, right_high, right_low, right_low], axis=0)
+            found = jnp.dot(stream, held, preferred_element_type=jnp.float32)
+            for n in range(2):
+                products[pl.ds(LEFT_SLOTS * (2 * quad + n), LEFT_SLOTS)] = (
+                    found[:, 2 * side * n : 2 * side * (n + 1)].reshape(LEFT_SLOTS, side, 2 * side))
+
+        def add(position, inner):
+            right_slot = right_lists[item, position]
+            source = LEFT_SLOTS * (right_slot >> 1) + left_lists[item, position]
+            sink = 2 * sink_lists[item, position] + (right_slot & 1)
+            sums[sink] += products[source]
+            return inner
+
+        lax.fori_loop(0, counts[item], add, 0)
+
+    @pl.when(section == SECTIONS - 1)
+    def _():
+        for sink in range(SINK_SLOTS):
+            total = sums[2 * sink] + pltpu.roll(sums[2 * sink + 1], side, 1)
+            out[pl.ds(sink * (side // 2), side // 2), :] = jnp.where(
+                low_lanes, total[: side // 2], pltpu.roll(total[side // 2 :], side, 1))
 
 
 def product_sums(left_lists, right_lists, sink_lists, counts, left_all, right_all):
     smem = pl.BlockSpec(memory_space=pltpu.SMEM)
-    vmem = pl.BlockSpec(memory_space=pltpu.VMEM)
     return pl.pallas_call(
         product_kernel,
-        out_shape=jax.ShapeDtypeStruct((SINK_SLOTS, TILE_SIDE, TILE_SIDE), jnp.float32),
-        in_specs=[smem] * 4 + [vmem] * 2,
-        out_specs=vmem,
+        out_shape=jax.ShapeDtypeStruct((SINK_SLOTS * TILE_SIDE // 2, 2 * TILE_SIDE), jnp.float32),
+        grid=(SECTIONS,),
+        in_specs=[smem] * 4 + [
+            pl.BlockSpec((1, LEFT_ROWS, 2 * TILE_SIDE), lambda section: (section, 0, 0)),
+            pl.BlockSpec((2, RIGHT_ROWS, 2 * TILE_SIDE), lambda section: (section, 0, 0)),
+        ],
+        out_specs=pl.BlockSpec((SINK_SLOTS * TILE_SIDE // 2, 2 * TILE_SIDE), lambda section: (0, 0)),
         scratch_shapes=[
             pltpu.VMEM((LEFT_SLOTS * RIGHT_SLOTS // 2, TILE_SIDE, 2 * TILE_SIDE), jnp.float32),
             pltpu.VMEM((2 * SINK_SLOTS, TILE_SIDE, 2 * TILE_SIDE), jnp.float32),
@@ -329,14 +353,13 @@
 
 
 def per_device(rows, cols, left_blocks, right_blocks, left_slots, right_slots, sink_slots, live_counts):
-    side = TILE_SIDE
-    right = right_blocks.reshape(RIGHT_SLOTS // 2, 2, side, side).transpose(0, 2, 1, 3).reshape(RIGHT_ROWS, 2 * side)
-    left = left_blocks.reshape(2, LEFT_ROWS, side).transpose(1, 0, 2).reshape(LEFT_ROWS, 2 * side)
+    right = right_blocks.reshape(RIGHT_ROWS, 2 * TILE_SIDE)
+    left = left_blocks.reshape(LEFT_ROWS, 2 * TILE_SIDE)
     left_all, right_all = exchange(rows, cols, left, right)
     total = product_sums(
         left_slots.reshape(PANELS, PRODUCTS), right_slots.reshape(PANELS, PRODUCTS),
         sink_slots.reshape(PANELS, PRODUCTS), live_counts.reshape(PANELS), left_all, right_all)
-    return total.reshape(1, 1, SINK_SLOTS, side * side)
+    return total.reshape(1, 1, SINK_SLOTS, TILE_SIDE * TILE_SIDE)
 
 
 def solution(mesh):

time: 84.2 us -> 80.4 us (0.955)
  local copies, waits for them, and re-layouts: 5.51 us -> 3.02 us
  other arithmetic: 1.81 us -> 0 us
    reshape x6 -> x1, local copies, waits for them, and re-layouts: 4.7 us -> 1.65 us  [per_device(): left = left_blocks.reshape(LEFT_ROWS, 2 * TILE_SIDE)]
    unnamed x1 -> x0, other arithmetic: 1.81 us -> none
where the time goes in v4:
time: 80.4 us; the launch traced here: 80.2 us
  Pallas kernels  77.2 us (96%)
  local copies, waits for them, and re-layouts  3.02 us (4%)
    pallas_call x1, Pallas kernels, exchange(): pl.pallas_call(functools.partial(exchange_kernel, rows, cols), out_shape=...  69.8 us
    pallas_call x1, Pallas kernels, product_sums(): pl.pallas_call(product_kernel, out_shape=jax.ShapeDtypeStruct((SINK_SLOTS...  7.35 us
    reshape x1, local copies, waits for them, and re-layouts, per_device(): left = left_blocks.reshape(LEFT_ROWS, 2 * TILE_SIDE)  1.65 us

profile of v4, /device:TPU:2, one launch (start us, length us, event | category | flops | bytes accessed | tf_op | source)
XLA Modules:
  0.0 80.2 jit_solution(2549828636223969505)
XLA Ops:
  0.0 0.8 copy.9
  0.8 0.6 reshape.24.counts
  1.4 1.6 %reshape.25.left_ref = f32[256,128]{1,0:T(8,128)} reshape(f32[1,2,4,4096]{3,2,1,0:T(4,128)} %param.6) | data formatting | bytes 262144 | tf_op jit(solution)/shard_map/reshape | solution.py:357
  3.0 69.8 %exchange.1 = (f32[4,256,128]{2,1,0:T(8,128)}, f32[8,640,128]{2,1,0:T(8,128)}) custom-call(f32[256,128]{1,0:T(8,128)} %reshape.25.left_ref, f32[640,128]{1,0:T(8,128)} %bitcast.5), custom_call_target="tpu_custom_call" | custom-call | tf_op jit(solution)/shard_map/exchange/pallas_call | solution.py:255
  72.9 7.3 %product_sums.1 = f32[384,128]{1,0:T(8,128)} custom-call(s32[8,24]{1,0:T(8,128)} %bitcast.6, s32[8,24]{1,0:T(8,128)} %bitcast.7, s32[8,24]{1,0:T(8,128)} %bitcast.8, s32[8]{0:T(128)} %reshape.24.counts, f32[4,256,128]{2,1,0:T(8,128)} %get-tuple-element.7.left_all, f32[8,640,128]{2,1,0:T(8,128)} %get-tuple-element.8.right_all), custom_call_target="tpu_custom_call" | custom-call | tf_op jit(solution)/shard_map/product_sums/pallas_call | solution.py:338

commit v5 on v4

--- a/solution.py
+++ b/solution.py
@@ -19,6 +19,9 @@
 RIGHT_ROWS = RIGHT_SLOTS * TILE_SIDE // 2
 CHUNK_ROWS = RIGHT_ROWS // CHUNKS
 TURNED = CHUNKS // 2
+DETOURS = PANELS - 2
+OFFSETS = (0, 0, 0, 6, 6, 6, 4, 2)
+TURNED_OFFSETS = (0, 6, 0, 6, 0, 6, 4, 2)
 MESH = pl.DeviceIdType.MESH
 
 
@@ -32,15 +35,15 @@
 
 def exchange_kernel(rows, cols, left_ref, right_ref, left_all, right_all, relay,
                     left_send, left_recv, entry_send, right_recv, down_send, up_send,
-                    relay_send, relay_recv):
+                    relay_send, relay_recv, detour, detour_send, detour_recv):
     row = lax.axis_index("row")
     column = lax.axis_index("col")
     parity = row % 2
     half_row = row // 2
     below = (row + rows - 1) % rows
     above = (row + 1) % rows
-    offset = chosen(column, (0, 0, 0, 6, 6, 6, 4, 2))
-    turned_offset = chosen(column, (0, 6, 0, 6, 0, 6, 4, 2))
+    offset = chosen(column, OFFSETS)
+    turned_offset = chosen(column, TURNED_OFFSETS)
     relay_shift = chosen(column, (0, rows - 4, 0, 0, 4, 0, 0, 0))
     relays = relay_shift != 0
     shift = (2 * column + offset) % rows
@@ -48,6 +51,18 @@
     moves = shift != 0
     greets_final = relays & (final_shift != relay_shift)
 
+    half = rows // 2
+    at_low = row % half == 0
+    at_high = row % half == half - 1
+    at_edge = at_low | at_high
+    y_low = column // 2 % 2
+    back_row = (row + half * (1 - y_low)) % rows
+    back_column = (column + 2 - 4 * y_low) % cols
+    ahead_row = (row + half * y_low) % rows
+    ahead_column = back_column
+    onto_row = (ahead_row + rows + 1 - 2 * at_low.astype(jnp.int32)) % rows
+    opposite_row = (ahead_row + (half - 1) * (at_low.astype(jnp.int32) - at_high.astype(jnp.int32)) + rows) % rows
+
     def greet(row_to, column_to):
         pl.semaphore_signal(barrier, inc=1, device_id=(row_to, column_to), device_id_type=MESH)
 
@@ -67,12 +82,18 @@
     def _():
         greet((row + final_shift) % rows, column)
 
+    @pl.when(at_edge)
+    def _():
+        greet(ahead_row, ahead_column)
+        greet(opposite_row, ahead_column)
+
     for section in range(SECTIONS):
         @pl.when((half_row + section) % cols != 0)
         def _():
             greet(row, (column + half_row + section) % cols)
 
     peers = 2 + moves.astype(jnp.int32) + relays.astype(jnp.int32) + greets_final.astype(jnp.int32)
+    peers += 2 * at_edge.astype(jnp.int32)
     for section in range(SECTIONS):
         peers += ((half_row + section) % cols != 0).astype(jnp.int32)
     pl.semaphore_wait(barrier, peers)
@@ -134,6 +155,53 @@
             recv_sem=right_recv.at[slot - 2 * parity, chunk],
             device_id=(above, column), device_id_type=MESH)
 
+    def start_down(slot, chunk):
+        odd = at_low & (chunk % 2 == 1)
+
+        @pl.when(odd)
+        def _():
+            detour_copy(slot, chunk, slot - entry_of(chunk), down_send).start()
+
+        @pl.when(jnp.logical_not(odd))
+        def _():
+            down_copy(slot, chunk).start()
+
+    def start_up(slot, chunk):
+        odd = at_high & (chunk % 2 == 1)
+
+        @pl.when(odd)
+        def _():
+            detour_copy(slot, chunk, entry_of(chunk) - slot, up_send).start()
+
+        @pl.when(jnp.logical_not(odd))
+        def _():
+            up_copy(slot, chunk).start()
+
+    def detour_copy(slot, chunk, place, send_sem):
+        return pltpu.make_async_remote_copy(
+            src_ref=right_all.at[slot, part(chunk)], dst_ref=detour.at[place, chunk // 2],
+            send_sem=send_sem.at[slot, chunk], recv_sem=detour_recv.at[place, chunk // 2],
+            device_id=(back_row, back_column), device_id_type=MESH)
+
+    ahead_offset = chosen(ahead_column, OFFSETS)
+    ahead_turned = chosen(ahead_column, TURNED_OFFSETS)
+    low = at_low.astype(jnp.int32)
+
+    def ahead_slot(chunk, place):
+        entry = parity + ahead_offset + (chunk < TURNED).astype(jnp.int32) * (ahead_turned - ahead_offset)
+        return entry + place * (2 * low - 1)
+
+    def passes(chunk, place):
+        slot = ahead_slot(chunk, place)
+        return at_edge & (chunk % 2 == 1) & (at_low & (slot <= PANELS - 3) | at_high & (slot >= 2))
+
+    def passed_copy(chunk, place):
+        slot = ahead_slot(chunk, place) + 2 * (2 * low - 1)
+        return pltpu.make_async_remote_copy(
+            src_ref=detour.at[place, chunk // 2], dst_ref=right_all.at[slot, part(chunk)],
+            send_sem=detour_send.at[place, chunk // 2], recv_sem=right_recv.at[slot, chunk],
+            device_id=(onto_row, ahead_column), device_id_type=MESH)
+
     for chunk in range(CHUNKS):
         direct = moves if chunk >= TURNED else moves & jnp.logical_not(relays)
 
@@ -172,11 +240,11 @@
 
         @pl.when(entry <= last_down)
         def _():
-            down_copy(entry, chunk).start()
+            start_down(entry, chunk)
 
         @pl.when(entry >= last_up)
         def _():
-            up_copy(entry, chunk).start()
+            start_up(entry, chunk)
         return carry
 
     lax.fori_loop(TURNED, CHUNKS, first, 0)
@@ -195,13 +263,20 @@
         higher = entry_of(chunk) + distance
         lower = entry_of(chunk) - distance
 
+        @pl.when(passes(chunk, distance - 1) & (distance <= DETOURS))
+        def _():
+            pltpu.make_async_copy(
+                right_ref.at[part(chunk)], detour.at[distance - 1, chunk // 2],
+                detour_recv.at[distance - 1, chunk // 2]).wait()
+            passed_copy(chunk, distance - 1).start()
+
         @pl.when(higher < PANELS)
         def _():
             arrived(higher, chunk)
 
         @pl.when(higher <= last_down)
         def _():
-            down_copy(higher, chunk).start()
+            start_down(higher, chunk)
 
         @pl.when(lower >= 0)
         def _():
@@ -209,10 +284,21 @@
 
         @pl.when(lower >= last_up)
         def _():
-            up_copy(lower, chunk).start()
+            start_up(lower, chunk)
         return carry
 
     lax.fori_loop(0, (PANELS - 1) * CHUNKS, onward, 0)
+
+    def passed(step, carry):
+        chunk = step % CHUNKS
+        place = step // CHUNKS
+
+        @pl.when(passes(chunk, place))
+        def _():
+            passed_copy(chunk, place).wait_send()
+        return carry
+
+    lax.fori_loop(0, DETOURS * CHUNKS, passed, 0)
 
     def sent(step, carry):
         slot = step // CHUNKS
@@ -264,6 +350,8 @@
             pltpu.VMEM((TURNED * CHUNK_ROWS, 2 * TILE_SIDE), jnp.float32),
             dma((SECTIONS,)), dma((SECTIONS,)), dma((CHUNKS,)), dma((PANELS, CHUNKS)),
             dma((PANELS, CHUNKS)), dma((PANELS, CHUNKS)), dma((TURNED,)), dma((TURNED,)),
+            pltpu.VMEM((DETOURS, CHUNKS // 2, CHUNK_ROWS, 2 * TILE_SIDE), jnp.float32),
+            dma((DETOURS, CHUNKS // 2)), dma((DETOURS, CHUNKS // 2)),
         ],
         compiler_params=pltpu.CompilerParams(collective_id=0, has_side_effects=True),
         name="exchange",

time: 80.4 us -> 105 us (1.31)
  the two profiles are of different devices: /device:TPU:2 before, /device:TPU:41 now
where the time goes in v5:
time: 105 us
  Pallas kernels  102 us (97%)
  local copies, waits for them, and re-layouts  3.02 us (3%)
    pallas_call x1, Pallas kernels, exchange(): pl.pallas_call(functools.partial(exchange_kernel, rows, cols), out_shape=...  94.2 us
    pallas_call x1, Pallas kernels, product_sums(): pl.pallas_call(product_kernel, out_shape=jax.ShapeDtypeStruct((SINK_SLOTS...  7.37 us

profile of v5, /device:TPU:41, one launch (start us, length us, event | category | flops | bytes accessed | tf_op | source)
XLA Modules:
  0.0 104.6 jit_solution(15275058928448640848)
XLA Ops:
  0.0 0.8 copy.9
  0.8 0.6 reshape.24.counts
  1.4 1.6 %reshape.25.left_ref = f32[256,128]{1,0:T(8,128)} reshape(f32[1,2,4,4096]{3,2,1,0:T(4,128)} %param.6) | data formatting | bytes 262144 | tf_op jit(solution)/shard_map/reshape | solution.py:445
  3.0 94.2 %exchange.1 = (f32[4,256,128]{2,1,0:T(8,128)}, f32[8,640,128]{2,1,0:T(8,128)}) custom-call(f32[256,128]{1,0:T(8,128)} %reshape.25.left_ref, f32[640,128]{1,0:T(8,128)} %bitcast.5), custom_call_target="tpu_custom_call" | custom-call | tf_op jit(solution)/shard_map/exchange/pallas_call | solution.py:341
  97.3 7.4 %product_sums.1 = f32[384,128]{1,0:T(8,128)} custom-call(s32[8,24]{1,0:T(8,128)} %bitcast.6, s32[8,24]{1,0:T(8,128)} %bitcast.7, s32[8,24]{1,0:T(8,128)} %bitcast.8, s32[8]{0:T(128)} %reshape.24.counts, f32[4,256,128]{2,1,0:T(8,128)} %get-tuple-element.7.left_all, f32[8,640,128]{2,1,0:T(8,128)} %get-tuple-element.8.right_all), custom_call_target="tpu_custom_call" | custom-call | tf_op jit(solution)/shard_map/product_sums/pallas_call | solution.py:426

commit v6 on v4

--- a/solution.py
+++ b/solution.py
@@ -32,7 +32,7 @@
 
 def exchange_kernel(rows, cols, left_ref, right_ref, left_all, right_all, relay,
                     left_send, left_recv, entry_send, right_recv, down_send, up_send,
-                    relay_send, relay_recv):
+                    relay_send, relay_recv, early_send):
     row = lax.axis_index("row")
     column = lax.axis_index("col")
     parity = row % 2
@@ -48,6 +48,12 @@
     moves = shift != 0
     greets_final = relays & (final_shift != relay_shift)
 
+    half = rows // 2
+    at_low = row % half == 0
+    at_high = row % half == half - 1
+    before_low = row % half == 1
+    before_high = row % half == half - 2
+
     def greet(row_to, column_to):
         pl.semaphore_signal(barrier, inc=1, device_id=(row_to, column_to), device_id_type=MESH)
 
@@ -67,12 +73,21 @@
     def _():
         greet((row + final_shift) % rows, column)
 
+    @pl.when(at_high)
+    def _():
+        greet((row + 2) % rows, column)
+
+    @pl.when(at_low)
+    def _():
+        greet((row + rows - 2) % rows, column)
+
     for section in range(SECTIONS):
         @pl.when((half_row + section) % cols != 0)
         def _():
             greet(row, (column + half_row + section) % cols)
 
     peers = 2 + moves.astype(jnp.int32) + relays.astype(jnp.int32) + greets_final.astype(jnp.int32)
+    peers += before_low.astype(jnp.int32) + before_high.astype(jnp.int32)
     for section in range(SECTIONS):
         peers += ((half_row + section) % cols != 0).astype(jnp.int32)
     pl.semaphore_wait(barrier, peers)
@@ -134,6 +149,29 @@
             recv_sem=right_recv.at[slot - 2 * parity, chunk],
             device_id=(above, column), device_id_type=MESH)
 
+    def early_copy(slot):
+        way = 1 - 2 * before_low.astype(jnp.int32)
+        onto = slot - 2 * way
+        return pltpu.make_async_remote_copy(
+            src_ref=right_all.at[slot, part(CHUNKS - 1)], dst_ref=right_all.at[onto, part(CHUNKS - 1)],
+            send_sem=early_send.at[slot], recv_sem=right_recv.at[onto, CHUNKS - 1],
+            device_id=((row + rows + 2 * way) % rows, column), device_id_type=MESH)
+
+    def sends_early(slot):
+        entry = entry_of(CHUNKS - 1)
+        return (before_low & (slot >= entry) & (slot <= PANELS - 3)) | (before_high & (slot <= entry) & (slot >= 2))
+
+    def sends_down(slot, chunk):
+        late = at_low & (chunk == CHUNKS - 1) & (slot != entry_of(chunk))
+        return (slot <= last_down) & jnp.logical_not(late)
+
+    def sends_up(slot, chunk):
+        late = at_high & (chunk == CHUNKS - 1) & (slot != entry_of(chunk))
+        return (slot >= last_up) & jnp.logical_not(late)
+
+    last_down = PANELS - 1 - 2 * (1 - parity)
+    last_up = 2 * parity
+
     for chunk in range(CHUNKS):
         direct = moves if chunk >= TURNED else moves & jnp.logical_not(relays)
 
@@ -159,9 +197,6 @@
         def _():
             left_local(section).start()
 
-    last_down = PANELS - 1 - 2 * (1 - parity)
-    last_up = 2 * parity
-
     def arrived(slot, chunk):
         pltpu.make_async_copy(
             right_ref.at[part(chunk)], right_all.at[slot, part(chunk)], right_recv.at[slot, chunk]).wait()
@@ -169,6 +204,10 @@
     def first(chunk, carry):
         entry = entry_of(chunk)
         arrived(entry, chunk)
+
+        @pl.when((chunk == CHUNKS - 1) & sends_early(entry))
+        def _():
+            early_copy(entry).start()
 
         @pl.when(entry <= last_down)
         def _():
@@ -199,7 +238,11 @@
         def _():
             arrived(higher, chunk)
 
-        @pl.when(higher <= last_down)
+        @pl.when((chunk == CHUNKS - 1) & (higher < PANELS) & sends_early(higher))
+        def _():
+            early_copy(higher).start()
+
+        @pl.when(sends_down(higher, chunk))
         def _():
             down_copy(higher, chunk).start()
 
@@ -207,7 +250,11 @@
         def _():
             arrived(lower, chunk)
 
-        @pl.when(lower >= last_up)
+        @pl.when((chunk == CHUNKS - 1) & (lower >= 0) & sends_early(lower))
+        def _():
+            early_copy(lower).start()
+
+        @pl.when(sends_up(lower, chunk))
         def _():
             up_copy(lower, chunk).start()
         return carry
@@ -219,13 +266,17 @@
         chunk = step % CHUNKS
         entry = entry_of(chunk)
 
-        @pl.when((slot >= entry) & (slot <= last_down))
+        @pl.when((slot >= entry) & sends_down(slot, chunk))
         def _():
             down_copy(slot, chunk).wait_send()
 
-        @pl.when((slot <= entry) & (slot >= last_up))
+        @pl.when((slot <= entry) & sends_up(slot, chunk))
         def _():
             up_copy(slot, chunk).wait_send()
+
+        @pl.when((chunk == CHUNKS - 1) & sends_early(slot))
+        def _():
+            early_copy(slot).wait_send()
         return carry
 
     lax.fori_loop(0, PANELS * CHUNKS, sent, 0)
@@ -263,7 +314,7 @@
         scratch_shapes=[
             pltpu.VMEM((TURNED * CHUNK_ROWS, 2 * TILE_SIDE), jnp.float32),
             dma((SECTIONS,)), dma((SECTIONS,)), dma((CHUNKS,)), dma((PANELS, CHUNKS)),
-            dma((PANELS, CHUNKS)), dma((PANELS, CHUNKS)), dma((TURNED,)), dma((TURNED,)),
+            dma((PANELS, CHUNKS)), dma((PANELS, CHUNKS)), dma((TURNED,)), dma((TURNED,)), dma((PANELS,)),
         ],
         compiler_params=pltpu.CompilerParams(collective_id=0, has_side_effects=True),
         name="exchange",

time: 80.4 us -> 90.6 us (1.13)
  the two profiles are of different devices: /device:TPU:2 before, /device:TPU:4 now
where the time goes in v6:
time: 90.6 us; the launch traced here: 90.4 us
  Pallas kernels  87.4 us (96%)
  local copies, waits for them, and re-layouts  3.02 us (3%)
    pallas_call x1, Pallas kernels, exchange(): pl.pallas_call(functools.partial(exchange_kernel, rows, cols), out_shape=...  79.6 us
    pallas_call x1, Pallas kernels, product_sums(): pl.pallas_call(product_kernel, out_shape=jax.ShapeDtypeStruct((SINK_SLOTS...  7.73 us

profile of v6, /device:TPU:4, one launch (start us, length us, event | category | flops | bytes accessed | tf_op | source)
XLA Modules:
  0.0 90.4 jit_solution(17744749033459683683)
XLA Ops:
  0.0 0.8 copy.9
  0.8 0.6 reshape.24.counts
  1.4 1.6 %reshape.25.left_ref = f32[256,128]{1,0:T(8,128)} reshape(f32[1,2,4,4096]{3,2,1,0:T(4,128)} %param.6) | data formatting | bytes 262144 | tf_op jit(solution)/shard_map/reshape | solution.py:408
  3.0 79.6 %exchange.1 = (f32[4,256,128]{2,1,0:T(8,128)}, f32[8,640,128]{2,1,0:T(8,128)}) custom-call(f32[256,128]{1,0:T(8,128)} %reshape.25.left_ref, f32[640,128]{1,0:T(8,128)} %bitcast.5), custom_call_target="tpu_custom_call" | custom-call | tf_op jit(solution)/shard_map/exchange/pallas_call | solution.py:306
  82.7 7.7 %product_sums.1 = f32[384,128]{1,0:T(8,128)} custom-call(s32[8,24]{1,0:T(8,128)} %bitcast.6, s32[8,24]{1,0:T(8,128)} %bitcast.7, s32[8,24]{1,0:T(8,128)} %bitcast.8, s32[8]{0:T(128)} %reshape.24.counts, f32[4,256,128]{2,1,0:T(8,128)} %get-tuple-element.7.left_all, f32[8,640,128]{2,1,0:T(8,128)} %get-tuple-element.8.right_all), custom_call_target="tpu_custom_call" | custom-call | tf_op jit(solution)/shard_map/product_sums/pallas_call | solution.py:389

commit v7 on v4

--- a/solution.py
+++ b/solution.py
@@ -288,7 +288,9 @@
     rows = LEFT_ROWS // 2
     low_lanes, low_lanes_left = ordered(side // 2), ordered(rows)
     for half in range(2):
-        left = left_all[0, pl.ds(half * rows, rows), :]
+        left = jnp.concatenate(
+            [left_all[0, pl.ds(half * rows + slot, side // 2, stride=LEFT_SLOTS), :] for slot in range(LEFT_SLOTS)],
+            axis=0)
         turned = pltpu.roll(left, side, 1)
         even = jnp.where(low_lanes_left, left, turned).reshape(LEFT_SLOTS, side // 2, 2 * side)
         odd = jnp.where(low_lanes_left, turned, left).reshape(LEFT_SLOTS, side // 2, 2 * side)
@@ -316,14 +318,18 @@
                 products[pl.ds(LEFT_SLOTS * (2 * quad + n), LEFT_SLOTS)] = (
                     found[:, 2 * side * n : 2 * side * (n + 1)].reshape(LEFT_SLOTS, side, 2 * side))
 
-        def add(position, inner):
+        def listed(position):
             right_slot = right_lists[item, position]
             source = LEFT_SLOTS * (right_slot >> 1) + left_lists[item, position]
-            sink = 2 * sink_lists[item, position] + (right_slot & 1)
+            return source, 2 * sink_lists[item, position] + (right_slot & 1)
+
+        def add(position, ahead):
+            source, sink = ahead
+            following = listed(jnp.minimum(position + 1, PRODUCTS - 1))
             sums[sink] += products[source]
-            return inner
-
-        lax.fori_loop(0, counts[item], add, 0)
+            return following
+
+        lax.fori_loop(0, counts[item], add, listed(0))
 
     @pl.when(section == SECTIONS - 1)
     def _():
@@ -354,7 +360,7 @@
 
 def per_device(rows, cols, left_blocks, right_blocks, left_slots, right_slots, sink_slots, live_counts):
     right = right_blocks.reshape(RIGHT_ROWS, 2 * TILE_SIDE)
-    left = left_blocks.reshape(LEFT_ROWS, 2 * TILE_SIDE)
+    left = left_blocks.reshape(2, LEFT_SLOTS, TILE_SIDE // 2, 2 * TILE_SIDE).transpose(0, 2, 1, 3).reshape(LEFT_ROWS, 2 * TILE_SIDE)
     left_all, right_all = exchange(rows, cols, left, right)
     total = product_sums(
         left_slots.reshape(PANELS, PRODUCTS), right_slots.reshape(PANELS, PRODUCTS),

time: 80.4 us -> 78.8 us (0.980)
  local copies, waits for them, and re-layouts: 3.02 us -> 1.37 us
    reshape x1 -> x0, local copies, waits for them, and re-layouts: 1.65 us -> none  [per_device(): left = left_blocks.reshape(LEFT_ROWS, 2 * TILE_SIDE)]
where the time goes in v7:
time: 78.8 us
  Pallas kernels  77.4 us (98%)
  local copies, waits for them, and re-layouts  1.37 us (2%)
    pallas_call x1, Pallas kernels, exchange(): pl.pallas_call(functools.partial(exchange_kernel, rows, cols), out_shape=...  69.8 us
    pallas_call x1, Pallas kernels, product_sums(): pl.pallas_call(product_kernel, out_shape=jax.ShapeDtypeStruct((SINK_SLOTS...  7.6 us

profile of v7, /device:TPU:2, one launch (start us, length us, event | category | flops | bytes accessed | tf_op | source)
XLA Modules:
  0.0 78.8 jit_solution(2968679433419222563)
XLA Ops:
  0.0 0.8 copy.10
  0.8 0.6 reshape.27.counts
  1.4 69.8 %exchange.1 = (f32[4,256,128]{2,1,0:T(8,128)}, f32[8,640,128]{2,1,0:T(8,128)}) custom-call(f32[256,128]{1,0:T(8,128)} %bitcast.11, f32[640,128]{1,0:T(8,128)} %bitcast.10), custom_call_target="tpu_custom_call" | custom-call | tf_op jit(solution)/shard_map/exchange/pallas_call | solution.py:255
  71.2 7.6 %product_sums.1 = f32[384,128]{1,0:T(8,128)} custom-call(s32[8,24]{1,0:T(8,128)} %bitcast.12, s32[8,24]{1,0:T(8,128)} %bitcast.13, s32[8,24]{1,0:T(8,128)} %bitcast.14, s32[8]{0:T(128)} %reshape.27.counts, f32[4,256,128]{2,1,0:T(8,128)} %get-tuple-element.7.left_all, f32[8,640,128]{2,1,0:T(8,128)} %get-tuple-element.8.right_all), custom_call_target="tpu_custom_call" | custom-call | tf_op jit(solution)/shard_map/product_sums/pallas_call | solution.py:344

commit v8 on v7

--- a/solution.py
+++ b/solution.py
@@ -39,8 +39,8 @@
     half_row = row // 2
     below = (row + rows - 1) % rows
     above = (row + 1) % rows
-    offset = chosen(column, (0, 0, 0, 6, 6, 6, 4, 2))
-    turned_offset = chosen(column, (0, 6, 0, 6, 0, 6, 4, 2))
+    offset = chosen(column, (0, 4, 0, 6, 2, 6, 2, 4))
+    turned_offset = chosen(column, (0, 6, 0, 6, 0, 6, 2, 4))
     relay_shift = chosen(column, (0, rows - 4, 0, 0, 4, 0, 0, 0))
     relays = relay_shift != 0
     shift = (2 * column + offset) % rows

time: 78.8 us -> 83.9 us (1.065)
  Pallas kernels: 77.4 us -> 82.3 us
    pallas_call x1, Pallas kernels: 69.8 us -> 74.7 us  [exchange(): pl.pallas_call(functools.partial(exchange_kernel, rows, cols), out_shape=...]
where the time goes in v8:
time: 83.9 us; the launch traced here: 83.7 us
  Pallas kernels  82.3 us (98%)
  local copies, waits for them, and re-layouts  1.37 us (2%)
    pallas_call x1, Pallas kernels, exchange(): pl.pallas_call(functools.partial(exchange_kernel, rows, cols), out_shape=...  74.7 us
    pallas_call x1, Pallas kernels, product_sums(): pl.pallas_call(product_kernel, out_shape=jax.ShapeDtypeStruct((SINK_SLOTS...  7.58 us

profile of v8, /device:TPU:2, one launch (start us, length us, event | category | flops | bytes accessed | tf_op | source)
XLA Modules:
  0.0 83.7 jit_solution(11289128485478870332)
XLA Ops:
  0.0 0.8 copy.10
  0.8 0.6 reshape.27.counts
  1.4 74.7 %exchange.1 = (f32[4,256,128]{2,1,0:T(8,128)}, f32[8,640,128]{2,1,0:T(8,128)}) custom-call(f32[256,128]{1,0:T(8,128)} %bitcast.11, f32[640,128]{1,0:T(8,128)} %bitcast.10), custom_call_target="tpu_custom_call" | custom-call | tf_op jit(solution)/shard_map/exchange/pallas_call | solution.py:255
  76.1 7.6 %product_sums.1 = f32[384,128]{1,0:T(8,128)} custom-call(s32[8,24]{1,0:T(8,128)} %bitcast.12, s32[8,24]{1,0:T(8,128)} %bitcast.13, s32[8,24]{1,0:T(8,128)} %bitcast.14, s32[8]{0:T(128)} %reshape.27.counts, f32[4,256,128]{2,1,0:T(8,128)} %get-tuple-element.7.left_all, f32[8,640,128]{2,1,0:T(8,128)} %get-tuple-element.8.right_all), custom_call_target="tpu_custom_call" | custom-call | tf_op jit(solution)/shard_map/product_sums/pallas_call | solution.py:344

commit v9 on v8

--- a/solution.py
+++ b/solution.py
@@ -18,7 +18,7 @@
 LEFT_ROWS = LEFT_SLOTS * TILE_SIDE
 RIGHT_ROWS = RIGHT_SLOTS * TILE_SIDE // 2
 CHUNK_ROWS = RIGHT_ROWS // CHUNKS
-TURNED = CHUNKS // 2
+TURNED = CHUNKS // 4
 MESH = pl.DeviceIdType.MESH
 
 

time: 83.9 us -> 87.9 us (1.048)
  the two profiles are of different devices: /device:TPU:2 before, /device:TPU:66 now
where the time goes in v9:
time: 87.9 us; the launch traced here: 87.7 us
  Pallas kernels  86.4 us (98%)
  local copies, waits for them, and re-layouts  1.37 us (2%)
    pallas_call x1, Pallas kernels, exchange(): pl.pallas_call(functools.partial(exchange_kernel, rows, cols), out_shape=...  78.8 us
    pallas_call x1, Pallas kernels, product_sums(): pl.pallas_call(product_kernel, out_shape=jax.ShapeDtypeStruct((SINK_SLOTS...  7.56 us

profile of v9, /device:TPU:66, one launch (start us, length us, event | category | flops | bytes accessed | tf_op | source)
XLA Modules:
  0.0 87.7 jit_solution(4778165286503472851)
XLA Ops:
  0.0 0.8 copy.10
  0.8 0.6 reshape.27.counts
  1.4 78.8 %exchange.1 = (f32[4,256,128]{2,1,0:T(8,128)}, f32[8,640,128]{2,1,0:T(8,128)}) custom-call(f32[256,128]{1,0:T(8,128)} %bitcast.11, f32[640,128]{1,0:T(8,128)} %bitcast.10), custom_call_target="tpu_custom_call" | custom-call | tf_op jit(solution)/shard_map/exchange/pallas_call | solution.py:255
  80.2 7.6 %product_sums.1 = f32[384,128]{1,0:T(8,128)} custom-call(s32[8,24]{1,0:T(8,128)} %bitcast.12, s32[8,24]{1,0:T(8,128)} %bitcast.13, s32[8,24]{1,0:T(8,128)} %bitcast.14, s32[8]{0:T(128)} %reshape.27.counts, f32[4,256,128]{2,1,0:T(8,128)} %get-tuple-element.7.left_all, f32[8,640,128]{2,1,0:T(8,128)} %get-tuple-element.8.right_all), custom_call_target="tpu_custom_call" | custom-call | tf_op jit(solution)/shard_map/product_sums/pallas_call | solution.py:344

commit v10 on v7

--- a/solution.py
+++ b/solution.py
@@ -18,7 +18,7 @@
 LEFT_ROWS = LEFT_SLOTS * TILE_SIDE
 RIGHT_ROWS = RIGHT_SLOTS * TILE_SIDE // 2
 CHUNK_ROWS = RIGHT_ROWS // CHUNKS
-TURNED = CHUNKS // 2
+TURNED = 3 * CHUNKS // 4
 MESH = pl.DeviceIdType.MESH
 
 

time: 78.8 us -> 84.1 us (1.067)
  Pallas kernels: 77.4 us -> 82.6 us
    pallas_call x1, Pallas kernels: 69.8 us -> 75.1 us  [exchange(): pl.pallas_call(functools.partial(exchange_kernel, rows, cols), out_shape=...]
where the time goes in v10:
time: 84.1 us; the launch traced here: 83.9 us
  Pallas kernels  82.6 us (98%)
  local copies, waits for them, and re-layouts  1.37 us (2%)
    pallas_call x1, Pallas kernels, exchange(): pl.pallas_call(functools.partial(exchange_kernel, rows, cols), out_shape=...  75.1 us
    pallas_call x1, Pallas kernels, product_sums(): pl.pallas_call(product_kernel, out_shape=jax.ShapeDtypeStruct((SINK_SLOTS...  7.51 us

profile of v10, /device:TPU:2, one launch (start us, length us, event | category | flops | bytes accessed | tf_op | source)
XLA Modules:
  0.0 83.9 jit_solution(7592602633969434616)
XLA Ops:
  0.0 0.8 copy.10
  0.8 0.6 reshape.27.counts
  1.4 75.1 %exchange.1 = (f32[4,256,128]{2,1,0:T(8,128)}, f32[8,640,128]{2,1,0:T(8,128)}) custom-call(f32[256,128]{1,0:T(8,128)} %bitcast.11, f32[640,128]{1,0:T(8,128)} %bitcast.10), custom_call_target="tpu_custom_call" | custom-call | tf_op jit(solution)/shard_map/exchange/pallas_call | solution.py:255
  76.4 7.5 %product_sums.1 = f32[384,128]{1,0:T(8,128)} custom-call(s32[8,24]{1,0:T(8,128)} %bitcast.12, s32[8,24]{1,0:T(8,128)} %bitcast.13, s32[8,24]{1,0:T(8,128)} %bitcast.14, s32[8]{0:T(128)} %reshape.27.counts, f32[4,256,128]{2,1,0:T(8,128)} %get-tuple-element.7.left_all, f32[8,640,128]{2,1,0:T(8,128)} %get-tuple-element.8.right_all), custom_call_target="tpu_custom_call" | custom-call | tf_op jit(solution)/shard_map/product_sums/pallas_call | solution.py:344

commit v11 on v7

--- a/solution.py
+++ b/solution.py
@@ -14,7 +14,7 @@
 PRODUCTS = 24
 SECTIONS = 4
 PANELS = 2 * SECTIONS
-CHUNKS = 4
+CHUNKS = 2
 LEFT_ROWS = LEFT_SLOTS * TILE_SIDE
 RIGHT_ROWS = RIGHT_SLOTS * TILE_SIDE // 2
 CHUNK_ROWS = RIGHT_ROWS // CHUNKS

time: 78.8 us -> 83.3 us (1.057)
  Pallas kernels: 77.4 us -> 81.8 us
    pallas_call x1, Pallas kernels: 69.8 us -> 74.2 us  [exchange(): pl.pallas_call(functools.partial(exchange_kernel, rows, cols), out_shape=...]
where the time goes in v11:
time: 83.3 us; the launch traced here: 83.2 us
  Pallas kernels  81.8 us (98%)
  local copies, waits for them, and re-layouts  1.37 us (2%)
    pallas_call x1, Pallas kernels, exchange(): pl.pallas_call(functools.partial(exchange_kernel, rows, cols), out_shape=...  74.2 us
    pallas_call x1, Pallas kernels, product_sums(): pl.pallas_call(product_kernel, out_shape=jax.ShapeDtypeStruct((SINK_SLOTS...  7.55 us

profile of v11, /device:TPU:2, one launch (start us, length us, event | category | flops | bytes accessed | tf_op | source)
XLA Modules:
  0.0 83.2 jit_solution(8513540103802976710)
XLA Ops:
  0.0 0.8 copy.10
  0.8 0.6 reshape.27.counts
  1.4 74.2 %exchange.1 = (f32[4,256,128]{2,1,0:T(8,128)}, f32[8,640,128]{2,1,0:T(8,128)}) custom-call(f32[256,128]{1,0:T(8,128)} %bitcast.11, f32[640,128]{1,0:T(8,128)} %bitcast.10), custom_call_target="tpu_custom_call" | custom-call | tf_op jit(solution)/shard_map/exchange/pallas_call | solution.py:255
  75.6 7.5 %product_sums.1 = f32[384,128]{1,0:T(8,128)} custom-call(s32[8,24]{1,0:T(8,128)} %bitcast.12, s32[8,24]{1,0:T(8,128)} %bitcast.13, s32[8,24]{1,0:T(8,128)} %bitcast.14, s32[8]{0:T(128)} %reshape.27.counts, f32[4,256,128]{2,1,0:T(8,128)} %get-tuple-element.7.left_all, f32[8,640,128]{2,1,0:T(8,128)} %get-tuple-element.8.right_all), custom_call_target="tpu_custom_call" | custom-call | tf_op jit(solution)/shard_map/product_sums/pallas_call | solution.py:344
